TPU v7x, 256 devices: a whole 4x4x8 slice. The times are simulated.
256 devices in a mesh: lat: 16 (over y_lo, x, core), lon: 16 (over y_hi, z).
Axes of the slice: x: 4, y: 4 (y_hi: 2, y_lo: 2; y = y_hi * 2 + y_lo), z: 8, core: 2. Of those that a mesh axis runs over, the one named last changes fastest.
Arguments:
- state: bfloat16 [64, 128, 4320], P(None, 'lat', 'lon'), may hold values from -6 to 6
- land_sea: int32 [128, 4320], P('lat', 'lon'), may hold values 0 or 1
- cotangent: bfloat16 [64, 128, 4320], P(None, 'lat', 'lon'), may hold values from -6 to 6
- kernel: float32 [64, 7, 7], replicated, may hold values from -0.875 to 0.875
- conv_bias: float32 [64], replicated, may hold values from -4 to 4
- ln_gain: float32 [64], replicated, may hold values from 0.1 to 1.9
- ln_bias: float32 [64], replicated, may hold values from -3 to 3
- w_expand: bfloat16 [64, 256], replicated, may hold values from -0.75 to 0.75
- b_expand: float32 [256], replicated, may hold values from -3 to 3
- w_project: bfloat16 [256, 64], replicated, may hold values from -0.375 to 0.375
Outputs:
- state_grad: bfloat16 [64, 128, 4320], P(None, 'lat', 'lon')
- kernel_grad: float32 [64, 7, 7], replicated
- conv_bias_grad: float32 [64], replicated
- gain_grad: float32 [64], replicated
- ln_bias_grad: float32 [64], replicated
- expand_grad: float32 [64, 256], replicated
- b_expand_grad: float32 [256], replicated
- project_grad: float32 [256, 64], replicated
- b_project_grad: float32 [64], replicated
Inputs may be any that keep to these rules, and one draw needn't show every extreme that they name: `land_sea`: 1 marks an ocean cell, 0 a land cell.
All inputs are finite; a program needn't handle non-finite values. No bound on the sum of `land_sea` on one device may be relied on, other than what follows from the above.
Results may differ from a plain program's by a relative error of at most 0.0064.
Values may be sent and summed in bfloat16 or wider, within the bound.
A program may use at most 64 MiB of HBM per device.

v0:
```python
import math

import jax
import jax.numpy as jnp
from jax import lax
from jax.sharding import PartitionSpec as P

TAPS = 7


ln_eps = 1e-06
root_half = 0.7071067811865476
inv_root_tau = 0.3989422804014327


def extended(shard, sides, width, wrap):
    for axis, dim in sides:
        size, length = (lax.axis_size(axis), shard.shape[dim])
        up = [(i, (i + 1) % size) for i in range(size if wrap else size - 1)]
        down = [(j, i) for i, j in up]
        last = lax.slice_in_dim(shard, length - width, length, axis=dim)
        first = lax.slice_in_dim(shard, 0, width, axis=dim)
        before = lax.ppermute(last, axis, up)
        after = lax.ppermute(first, axis, down)
        shard = jnp.concatenate([before, shard, after], axis=dim)
    return shard


def gelu_value(values):
    return 0.5 * values * (1.0 + lax.erf(values * root_half))


def gelu_slope(values):
    return (
        0.5 * (1.0 + lax.erf(values * root_half))
        + values * jnp.exp(-0.5 * values * values) * inv_root_tau
    )


def extend_in(field, rim_width):
    row_rim = extended(field, (("lat", 1),), rim_width, False)
    return extended(row_rim, (("lon", 2),), rim_width, True)


def extend_back(field):
    row_rim = extended(field, (("lat", 1),), 3, False)
    return extended(row_rim, (("lon", 2),), 3, True)


def depthwise(padded, kernel, n_rows, n_cols):
    total = jnp.zeros((padded.shape[0], n_rows, n_cols), jnp.float32)
    for row_tap in range(TAPS):
        for col_tap in range(TAPS):
            total = (
                total
                + kernel[:, row_tap, col_tap][:, None, None]
                * padded[:, row_tap : row_tap + n_rows, col_tap : col_tap + n_cols]
            )
    return total


def transpose_conv(padded, kernel, n_rows, n_cols):
    total = jnp.zeros((padded.shape[0], n_rows, n_cols), jnp.float32)
    for row_tap in range(TAPS):
        for col_tap in range(TAPS):
            total = (
                total
                + kernel[:, row_tap, col_tap][:, None, None]
                * padded[:, 6 - row_tap : 6 - row_tap + n_rows, 6 - col_tap : 6 - col_tap + n_cols]
            )
    return total


def kernel_sums(dconv, padded, n_rows, n_cols):
    taps = []
    for row_tap in range(TAPS):
        for col_tap in range(TAPS):
            taps.append(
                jnp.sum(
                    dconv * padded[:, row_tap : row_tap + n_rows, col_tap : col_tap + n_cols],
                    axis=(1, 2),
                )
            )
    return jnp.stack(taps, axis=1).reshape(dconv.shape[0], TAPS, TAPS)


def cell_terms(conv_out, wet_cot, ln_gain, ln_bias, w_expand, b_expand, w_project):
    center = conv_out - jnp.mean(conv_out, axis=0, keepdims=True)
    rstd = lax.rsqrt(jnp.mean(center * center, axis=0, keepdims=True) + ln_eps)
    normed = center * rstd
    zed = (normed * ln_gain[:, None, None] + ln_bias[:, None, None]).astype(jnp.bfloat16)
    pre = (
        jnp.einsum("chw,ce->ehw", zed, w_expand, preferred_element_type=jnp.float32)
        + b_expand[:, None, None]
    )
    act = gelu_value(pre).astype(jnp.bfloat16)
    dact = jnp.einsum("chw,ec->ehw", wet_cot, w_project, preferred_element_type=jnp.float32)
    dhid = (dact * gelu_slope(pre)).astype(jnp.bfloat16)
    dzed = jnp.einsum("ehw,ce->chw", dhid, w_expand, preferred_element_type=jnp.float32)
    dnorm = dzed * ln_gain[:, None, None]
    dconv = rstd * (
        dnorm
        - jnp.mean(dnorm, axis=0, keepdims=True)
        - normed * jnp.mean(dnorm * normed, axis=0, keepdims=True)
    )
    return (zed, act, dhid, normed, dzed, dconv)


def pointwise_sums(zed, act, dhid, normed, dzed, wet_cot):
    expand_sum = jnp.einsum("chw,ehw->ce", zed, dhid, preferred_element_type=jnp.float32)
    b_expand_sum = jnp.sum(dhid.astype(jnp.float32), axis=(1, 2))
    project_sum = jnp.einsum("ehw,chw->ec", act, wet_cot, preferred_element_type=jnp.float32)
    b_project_sum = jnp.sum(wet_cot.astype(jnp.float32), axis=(1, 2))
    gain_sum = jnp.sum(dzed * normed, axis=(1, 2))
    bias_sum = jnp.sum(dzed, axis=(1, 2))
    return (expand_sum, b_expand_sum, project_sum, b_project_sum, gain_sum, bias_sum)


def body(
    state, land_sea, cotangent, kernel, conv_bias, ln_gain, ln_bias, w_expand, b_expand, w_project
):
    n_chan, n_rows, n_cols = state.shape
    wet_cot = cotangent * land_sea[None].astype(jnp.bfloat16)
    state_ext = extend_in(state, 3).astype(jnp.float32)
    conv_out = depthwise(state_ext, kernel, n_rows, n_cols) + conv_bias[:, None, None]
    terms = cell_terms(conv_out, wet_cot, ln_gain, ln_bias, w_expand, b_expand, w_project)
    point = pointwise_sums(terms[0], terms[1], terms[2], terms[3], terms[4], wet_cot)
    dconv = terms[5]
    dconv_ext = extend_back(dconv)
    tap_sum = kernel_sums(dconv, state_ext, n_rows, n_cols)
    bias_conv_sum = jnp.sum(dconv, axis=(1, 2))
    totals = lax.psum(
        (point[0], point[1], point[2], point[3], point[4], point[5], tap_sum, bias_conv_sum),
        ("lat", "lon"),
    )
    state_grad = (
        cotangent.astype(jnp.float32) + transpose_conv(dconv_ext, kernel, n_rows, n_cols)
    ).astype(jnp.bfloat16)
    scale = 1.0 / math.sqrt(n_rows * lax.axis_size("lat") * n_cols * lax.axis_size("lon"))
    return (
        state_grad,
        totals[6] * scale,
        totals[7] * scale,
        totals[4] * scale,
        totals[5] * scale,
        totals[0] * scale,
        totals[1] * scale,
        totals[2] * scale,
        totals[3] * scale,
    )


def solution(mesh):
    in_specs = (
        P(None, "lat", "lon"),
        P("lat", "lon"),
        P(None, "lat", "lon"),
        P(),
        P(),
        P(),
        P(),
        P(),
        P(),
        P(),
    )
    out_specs = (P(None, "lat", "lon"), P(), P(), P(), P(), P(), P(), P(), P())
    return jax.shard_map(body, mesh=mesh, in_specs=in_specs, out_specs=out_specs, check_vma=False)
```

profile of v0, /device:TPU:1, one launch (start us, length us, event | category | flops | bytes accessed | tf_op | source)
XLA Modules:
  0.0 423.0 jit_solution(17317879681181171491)
XLA Ops:
  7.3 1.4 fusion.87
  8.7 4.5 %collective-permute-start = (bf16[64,3,270]{2,0,1:T(8,128)(2,1)S(1)}, bf16[64,3,270]{2,0,1:T(8,128)(2,1)S(1)}, u32[]{:S(2)}, u32[]{:S(2)}) collective-permute-start(bf16[64,3,270]{2,0,1:T(8,128)(2,1)S(1)} %copy.32), channel_id=1, source_target_pairs={{0,16},{16,32},{32,48},{48,64},{64,80},{80,96},{96,112},{112,128},... | collective-permute-start | bytes 311048 | tf_op jit(solution)/shard_map/ppermute | solution.py:23
  13.2 1.9 collective-permute-start.1
  15.2 1.1 convert_reduce_fusion.1
  16.4 3.3 collective-permute-done.1
  19.9 2.0 collective-permute-start.2
  21.9 6.7 %collective-permute-start.3 = (bf16[64,14,3]{2,0,1:T(8,128)(2,1)S(1)}, bf16[64,14,3]{2,0,1:T(8,128)(2,1)S(1)}, u32[]{:S(2)}, u32[]{:S(2)}) collective-permute-start(bf16[64,14,3]{2,0,1:T(8,128)(2,1)S(1)} %get-tuple-element.91), channel_id=1, source_target_pairs={{1,0},{2,1},{3,2},{4,3},{5,4},{6,5},{7,6},{8,7},{9,8},{10,9},{11,1... | collective-permute-start | bytes 16136 | tf_op jit(solution)/shard_map/ppermute | solution.py:24
  28.6 3.2 collective-permute-done.2
  32.3 9.7 %fusion.84 = (f32[8,270]{1,0:T(8,128)S(1)}, f32[64,8,270]{2,0,1:T(8,128)S(1)}) fusion(f32[64]{0:T(128)S(1)} %copy-done.56, f32[64,14,276]{2,0,1:T(8,128)S(1)} %maximum_convert_fusion, f32[64]{0:T(128)S(1)} %get-tuple-element.141, f32[64]{0:T(128)S(1)} %get-tuple-element.142, f32[64]{0:T(128)S(1)} %get-tuple-element.95, f32[64]{0:T(128)S(1)} %get-tuple-element.96, ...), kind=kLoop, calls=%fused_computation.269 | loop fusion | flops 13683600 | bytes 27669440 | tf_op jit(solution)/shard_map/reduce_sum | solution.py:88
  42.3 0.6 fusion.79
  43.0 1.3 convolution_bitcast_fusion
  44.3 1.9 convert_reduce_fusion
  46.2 1.0 copy-done.3
  47.2 1.0 convolution_bitcast_fusion.1
  48.2 2.4 fusion.72
  50.7 4.6 %multiply_reduce_fusion = (f32[64]{0:T(128)}, f32[64]{0:T(128)}, f32[64]{0:T(128)}, f32[64]{0:T(128)}, f32[64]{0:T(128)}, /*index=5*/f32[64]{0:T(128)}, f32[64]{...) fusion(f32[64,14,276]{2,0,1:T(8,128)S(1)} %maximum_convert_fusi, ...), kind=kLoop, calls=%fused_computation.135 | loop fusion | flops 5943168 | bytes 11651584 | tf_op jit(solution)/shard_map/reduce_sum | solution.py:79
  55.2 2.6 multiply_reduce_fusion.36
  57.9 4.0 multiply_reduce_fusion.18
  62.2 0.9 copy-done.2
  63.5 78.1 %all-reduce = (f32[64,7,7]{0,2,1:T(8,128)S(1)}, f32[64]{0:T(128)S(1)}, f32[64]{0:T(128)S(1)}, f32[64]{0:T(128)S(1)}, f32[256]{0:T(256)S(1)}, /*index=5*/f32[64]{0:T(128)S(1)}) all-reduce(f32[64,7,7]{0,2,1:T(8,128)S(1)} %reshape.47, f32[64]{0:T(128)S(1)} %get-tuple-element.70, ...), channel_id=1, replica_groups=mesh['lat'=16,'lon'=16] {'lat','lon'}, use_global_device_ids=true, to_apply=%region_53.0 | all-reduce | flops 3648 | bytes 29184 | tf_op jit(solution)/shard_map/psum | solution.py:132
  141.7 0.6 broadcast_multiply_fusion.3
  144.9 3.8 collective-permute-start.4
  148.7 1.9 collective-permute-start.5
  150.7 234.3 %all-reduce.4.cloned.1.call-done = (f32[64,256]{1,0:T(8,128)}, f32[256,64]{0,1:T(8,128)}) async-done(((f32[64,256]{1,0:T(8,128)}, f32[256,64]{0,1:T(8,128)}), (f32[64,256]{1,0:T(8,128)}, f32[256,64]{0,1:T(8,128)})) %all-reduce.4.cloned.1.call-update) | async-done | bytes 131088 | tf_op jit(solution)/shard_map/psum | solution.py:132
  385.0 1.5 broadcast_multiply_fusion.2
  386.7 3.6 collective-permute-start.6
  390.3 0.6 broadcast_multiply_fusion.1
  391.0 9.4 %collective-permute-done.6 = f32[64,14,3]{2,0,1:T(8,128)S(1)} collective-permute-done((f32[64,14,3]{2,0,1:T(8,128)S(1)}, f32[64,14,3]{2,0,1:T(8,128)S(1)}, u32[]{:S(2)}, u32[]{:S(2)}) %collective-permute-start.6) | collective-permute-done | bytes 10784 | tf_op jit(solution)/shard_map/ppermute | solution.py:24
  400.4 6.0 %collective-permute-done.7 = f32[64,14,3]{2,0,1:T(8,128)S(1)} collective-permute-done((f32[64,14,3]{2,0,1:T(8,128)S(1)}, f32[64,14,3]{2,0,1:T(8,128)S(1)}, u32[]{:S(2)}, u32[]{:S(2)}) %collective-permute-start.7) | collective-permute-done | bytes 10784 | tf_op jit(solution)/shard_map/ppermute | solution.py:23
  406.4 0.6 pad_maximum_fusion
  407.1 8.1 %fusion.73 = bf16[64,8,270]{2,0,1:T(8,128)(2,1)S(1)} fusion(f32[64,14,273]{2,0,1:T(8,128)S(1)} %get-tuple-element.85, f32[64,8,270]{2,0,1:T(8,128)S(1)} %get-tuple-element.81, f32[64,3,270]{2,0,1:T(8,128)S(1)} %collective-permute-done.4, f32[64,14,273]{2,0,1:T(8,128)S(1)} %get-tuple-element.84, f32[64,3,270]{2,0,1:T(8,128)S(1)} %collective-permute-done.5, ...), kind=kLoop, calls=%fused_computation.189 | loop fusion | flops 14653440 | bytes 24757504 | tf_op jit(solution)/shard_map/convert_element_type | solution.py:138
  415.2 1.0 copy.25
  (148 shorter events, 4.4 us)
Async XLA Ops:
  7.2 35.1 %copy-start = (bf16[64,256]{1,0:T(8,128)(2,1)S(1)}, bf16[64,256]{1,0:T(8,128)(2,1)}, u32[]{:S(2)}) copy-start(bf16[64,256]{1,0:T(8,128)(2,1)} %param.17) | copy-start | bytes 98308
  7.2 377.7 %all-reduce.4.cloned.1.call-start = ((), (), s32[]{:S(2)}) async-start(), calls=%async_computation | async-start | bytes 262144 | tf_op jit(solution)/shard_map/psum | solution.py:132
  8.7 7.6 %collective-permute-start = (bf16[64,3,270]{2,0,1:T(8,128)(2,1)S(1)}, bf16[64,3,270]{2,0,1:T(8,128)(2,1)S(1)}, u32[]{:S(2)}, u32[]{:S(2)}) collective-permute-start(bf16[64,3,270]{2,0,1:T(8,128)(2,1)S(1)} %copy.32), channel_id=1, source_target_pairs={{0,16},{16,32},{32,48},{48,64},{64,80},{80,96},{96,112},{112,128},... | collective-permute-start | bytes 311048 | tf_op jit(solution)/shard_map/ppermute | solution.py:23
  13.2 6.5 %collective-permute-start.1 = (bf16[64,3,270]{2,0,1:T(8,128)(2,1)S(1)}, bf16[64,3,270]{2,0,1:T(8,128)(2,1)S(1)}, u32[]{:S(2)}, u32[]{:S(2)}) collective-permute-start(bf16[64,3,270]{2,0,1:T(8,128)(2,1)S(1)} %copy.33), channel_id=1, source_target_pairs={{16,0},{32,16},{48,32},{64,48},{80,64},{96,80},{112,96},{128,112},... | collective-permute-start | bytes 311048 | tf_op jit(solution)/shard_map/ppermute | solution.py:24
  16.3 16.0 %copy-start.10 = (f32[64]{0:T(128)}, f32[64]{0:T(128)S(1)}, u32[]{:S(2)}) copy-start(f32[64]{0:T(128)S(1)} %get-tuple-element.131) | copy-start | bytes 772
  19.9 12.0 %collective-permute-start.2 = (bf16[64,14,3]{2,0,1:T(8,128)(2,1)S(1)}, bf16[64,14,3]{2,0,1:T(8,128)(2,1)S(1)}, u32[]{:S(2)}, u32[]{:S(2)}) collective-permute-start(bf16[64,14,3]{2,0,1:T(8,128)(2,1)S(1)} %get-tuple-element.90), channel_id=1, source_target_pairs={{0,1},{1,2},{2,3},{3,4},{4,5},{5,6},{6,7},{7,8},{8,9},{9,10},{10,1... | collective-permute-start | bytes 16136 | tf_op jit(solution)/shard_map/ppermute | solution.py:23
  21.9 10.0 %collective-permute-start.3 = (bf16[64,14,3]{2,0,1:T(8,128)(2,1)S(1)}, bf16[64,14,3]{2,0,1:T(8,128)(2,1)S(1)}, u32[]{:S(2)}, u32[]{:S(2)}) collective-permute-start(bf16[64,14,3]{2,0,1:T(8,128)(2,1)S(1)} %get-tuple-element.91), channel_id=1, source_target_pairs={{1,0},{2,1},{3,2},{4,3},{5,4},{6,5},{7,6},{8,7},{9,8},{10,9},{11,1... | collective-permute-start | bytes 16136 | tf_op jit(solution)/shard_map/ppermute | solution.py:24
  28.5 13.5 %copy-start.14 = (f32[64]{0:T(128)}, f32[64]{0:T(128)S(1)}, u32[]{:S(2)}) copy-start(f32[64]{0:T(128)S(1)} %get-tuple-element.133) | copy-start | bytes 772
  28.5 13.5 %copy-start.16 = (f32[64]{0:T(128)}, f32[64]{0:T(128)S(1)}, u32[]{:S(2)}) copy-start(f32[64]{0:T(128)S(1)} %get-tuple-element.134) | copy-start | bytes 772
  28.6 13.5 %copy-start.18 = (f32[64]{0:T(128)}, f32[64]{0:T(128)S(1)}, u32[]{:S(2)}) copy-start(f32[64]{0:T(128)S(1)} %get-tuple-element.135) | copy-start | bytes 772
  28.6 13.5 %copy-start.20 = (f32[64]{0:T(128)}, f32[64]{0:T(128)S(1)}, u32[]{:S(2)}) copy-start(f32[64]{0:T(128)S(1)} %get-tuple-element.136) | copy-start | bytes 772
  28.6 13.5 %copy-start.22 = (f32[64]{0:T(128)}, f32[64]{0:T(128)S(1)}, u32[]{:S(2)}) copy-start(f32[64]{0:T(128)S(1)} %get-tuple-element.137) | copy-start | bytes 772
  28.6 13.5 %copy-start.24 = (f32[64]{0:T(128)}, f32[64]{0:T(128)S(1)}, u32[]{:S(2)}) copy-start(f32[64]{0:T(128)S(1)} %get-tuple-element.138) | copy-start | bytes 772
  28.6 13.5 %copy-start.26 = (f32[64]{0:T(128)}, f32[64]{0:T(128)S(1)}, u32[]{:S(2)}) copy-start(f32[64]{0:T(128)S(1)} %get-tuple-element.139) | copy-start | bytes 772
  28.6 13.5 %copy-start.28 = (f32[64]{0:T(128)}, f32[64]{0:T(128)S(1)}, u32[]{:S(2)}) copy-start(f32[64]{0:T(128)S(1)} %get-tuple-element.140) | copy-start | bytes 772
  28.6 13.5 %copy-start.30 = (f32[64]{0:T(128)}, f32[64]{0:T(128)S(1)}, u32[]{:S(2)}) copy-start(f32[64]{0:T(128)S(1)} %get-tuple-element.141) | copy-start | bytes 772
  144.9 241.6 %collective-permute-start.4 = (f32[64,3,270]{2,0,1:T(8,128)S(1)}, f32[64,3,270]{2,0,1:T(8,128)S(1)}, u32[]{:S(2)}, u32[]{:S(2)}) collective-permute-start(f32[64,3,270]{2,0,1:T(8,128)S(1)} %get-tuple-element.88), channel_id=1, source_target_pairs={{0,16},{16,32},{32,48},{48,64},{64,80},{80,96},{96,112},{112,128},... | collective-permute-start | bytes 622088 | tf_op jit(solution)/shard_map/ppermute | solution.py:23
  148.7 237.7 %collective-permute-start.5 = (f32[64,3,270]{2,0,1:T(8,128)S(1)}, f32[64,3,270]{2,0,1:T(8,128)S(1)}, u32[]{:S(2)}, u32[]{:S(2)}) collective-permute-start(f32[64,3,270]{2,0,1:T(8,128)S(1)} %get-tuple-element.89), channel_id=1, source_target_pairs={{16,0},{32,16},{48,32},{64,48},{80,64},{96,80},{112,96},{128,112},... | collective-permute-start | bytes 622088 | tf_op jit(solution)/shard_map/ppermute | solution.py:24
  386.7 13.7 %collective-permute-start.6 = (f32[64,14,3]{2,0,1:T(8,128)S(1)}, f32[64,14,3]{2,0,1:T(8,128)S(1)}, u32[]{:S(2)}, u32[]{:S(2)}) collective-permute-start(f32[64,14,3]{2,0,1:T(8,128)S(1)} %get-tuple-element.86), channel_id=1, source_target_pairs={{1,0},{2,1},{3,2},{4,3},{5,4},{6,5},{7,6},{8,7},{9,8},{10,9},{11,1... | collective-permute-start | bytes 32264 | tf_op jit(solution)/shard_map/ppermute | solution.py:24
  390.3 16.1 %collective-permute-start.7 = (f32[64,14,3]{2,0,1:T(8,128)S(1)}, f32[64,14,3]{2,0,1:T(8,128)S(1)}, u32[]{:S(2)}, u32[]{:S(2)}) collective-permute-start(f32[64,14,3]{2,0,1:T(8,128)S(1)} %get-tuple-element.87), channel_id=1, source_target_pairs={{0,1},{1,2},{2,3},{3,4},{4,5},{5,6},{6,7},{7,8},{8,9},{9,10},{10,1... | collective-permute-start | bytes 32264 | tf_op jit(solution)/shard_map/ppermute | solution.py:23
  390.9 16.1 %copy-start.11 = (f32[64]{0:T(128)S(1)}, f32[64]{0:T(128)}, u32[]{:S(2)}) copy-start(f32[64]{0:T(128)} %copy-done.10) | copy-start | bytes 772
  390.9 16.1 %copy-start.13 = (f32[64]{0:T(128)S(1)}, f32[64]{0:T(128)}, u32[]{:S(2)}) copy-start(f32[64]{0:T(128)} %copy-done.12) | copy-start | bytes 772
  390.9 16.1 %copy-start.15 = (f32[64]{0:T(128)S(1)}, f32[64]{0:T(128)}, u32[]{:S(2)}) copy-start(f32[64]{0:T(128)} %copy-done.14) | copy-start | bytes 772
  390.9 16.1 %copy-start.17 = (f32[64]{0:T(128)S(1)}, f32[64]{0:T(128)}, u32[]{:S(2)}) copy-start(f32[64]{0:T(128)} %copy-done.16) | copy-start | bytes 772
  390.9 16.1 %copy-start.19 = (f32[64]{0:T(128)S(1)}, f32[64]{0:T(128)}, u32[]{:S(2)}) copy-start(f32[64]{0:T(128)} %copy-done.18) | copy-start | bytes 772
  391.0 16.1 %copy-start.21 = (f32[64]{0:T(128)S(1)}, f32[64]{0:T(128)}, u32[]{:S(2)}) copy-start(f32[64]{0:T(128)} %copy-done.20) | copy-start | bytes 772
  391.0 16.1 %copy-start.23 = (f32[64]{0:T(128)S(1)}, f32[64]{0:T(128)}, u32[]{:S(2)}) copy-start(f32[64]{0:T(128)} %copy-done.22) | copy-start | bytes 772
  391.0 16.1 %copy-start.25 = (f32[64]{0:T(128)S(1)}, f32[64]{0:T(128)}, u32[]{:S(2)}) copy-start(f32[64]{0:T(128)} %copy-done.24) | copy-start | bytes 772
  391.0 16.1 %copy-start.27 = (f32[64]{0:T(128)S(1)}, f32[64]{0:T(128)}, u32[]{:S(2)}) copy-start(f32[64]{0:T(128)} %copy-done.26) | copy-start | bytes 772
  391.0 16.1 %copy-start.29 = (f32[64]{0:T(128)S(1)}, f32[64]{0:T(128)}, u32[]{:S(2)}) copy-start(f32[64]{0:T(128)} %copy-done.28) | copy-start | bytes 772
  391.0 16.1 %copy-start.31 = (f32[64]{0:T(128)S(1)}, f32[64]{0:T(128)}, u32[]{:S(2)}) copy-start(f32[64]{0:T(128)} %copy-done.30) | copy-start | bytes 772
  391.0 16.1 %copy-start.33 = (f32[64]{0:T(128)S(1)}, f32[64]{0:T(128)}, u32[]{:S(2)}) copy-start(f32[64]{0:T(128)} %copy-done.32) | copy-start | bytes 772
  (36 other events, 133.4 us)
Sparse Core Ops, SparseCore 0:
  144.5 240.3 all-reduce.3
where the time goes:
time: 423 us
  waiting for transfers between devices  256 us (61%)
  blocking collectives  78.1 us (18%)
  other arithmetic  36.9 us (9%)
  starting transfers between devices  24.5 us (6%)
  between operations  15 us (4%)
  matrix products  7.29 us (2%)
  local copies, waits for them, and re-layouts  5.06 us (1%)
    psum x1, waiting for transfers between devices, body(): lax.psum((point[0], point[1], point[2], point[3], point[4], point[5], tap...  234 us
    psum x1, blocking collectives, body(): lax.psum((point[0], point[1], point[2], point[3], point[4], point[5], tap...  78.1 us
    ppermute x4, starting transfers between devices, extended(): after = lax.ppermute(first, axis, down)  14.1 us
    ppermute x4, waiting for transfers between devices, extended(): after = lax.ppermute(first, axis, down)  12.6 us
    reduce_sum x3, other arithmetic, kernel_sums(): jnp.sum(dconv * padded[:, row_tap:row_tap + n_rows, col_tap:col_tap + n_c...  11.2 us
    ppermute x4, starting transfers between devices, extended(): before = lax.ppermute(last, axis, up)  10.3 us
    reduce_sum x1, other arithmetic, cell_terms(): center = conv_out - jnp.mean(conv_out, axis=0, keepdims=True)  9.69 us
    ppermute x4, waiting for transfers between devices, extended(): before = lax.ppermute(last, axis, up)  9.23 us
  transfers between devices with their start and end apart: 9, of which 5 were waited for; matrix products, arithmetic and copies ran while one was open for 1% of the time, Pallas kernels for 0%

commit v1 on v0

--- a/solution.py
+++ b/solution.py
@@ -3,6 +3,8 @@
 import jax
 import jax.numpy as jnp
 from jax import lax
+from jax.experimental import pallas as pl
+from jax.experimental.pallas import tpu as pltpu
 from jax.sharding import PartitionSpec as P
 
 TAPS = 7
@@ -114,6 +116,102 @@
     gain_sum = jnp.sum(dzed * normed, axis=(1, 2))
     bias_sum = jnp.sum(dzed, axis=(1, 2))
     return (expand_sum, b_expand_sum, project_sum, b_project_sum, gain_sum, bias_sum)
+
+
+N_GROUP = 16
+CHUNK = 18
+MESH = pl.DeviceIdType.MESH
+
+
+def reduce_kernel(x_ref, o_ref, part, gather, s1, r1, s2, r2, s3, r3):
+    la = lax.axis_index("lat")
+    lo = lax.axis_index("lon")
+
+    def lat_peer(k):
+        return {"lat": lax.rem(la + k, N_GROUP), "lon": lo}
+
+    def lon_peer(k):
+        return {"lat": la, "lon": lax.rem(lo + k, N_GROUP)}
+
+    barrier = pltpu.get_barrier_semaphore()
+    for k in range(1, N_GROUP):
+        pl.semaphore_signal(barrier, inc=1, device_id=lat_peer(k), device_id_type=MESH)
+        pl.semaphore_signal(barrier, inc=1, device_id=lon_peer(k), device_id_type=MESH)
+    pl.semaphore_wait(barrier, 2 * (N_GROUP - 1))
+
+    copies = []
+    for k in range(1, N_GROUP):
+        copy = pltpu.make_async_remote_copy(
+            src_ref=x_ref.at[lax.rem(la + k, N_GROUP)],
+            dst_ref=part.at[k],
+            send_sem=s1.at[k],
+            recv_sem=r1.at[k],
+            device_id=lat_peer(k),
+            device_id_type=MESH,
+        )
+        copy.start()
+        copies.append(copy)
+    total = x_ref[la]
+    for k in range(1, N_GROUP):
+        copies[k - 1].wait()
+        total = total + part[k]
+    gather[lo] = total
+
+    copies = []
+    for k in range(1, N_GROUP):
+        copy = pltpu.make_async_remote_copy(
+            src_ref=gather.at[lo],
+            dst_ref=gather.at[lo],
+            send_sem=s2.at[k],
+            recv_sem=r2.at[k],
+            device_id=lon_peer(k),
+            device_id_type=MESH,
+        )
+        copy.start()
+        copies.append(copy)
+    for copy in copies:
+        copy.wait()
+    total = gather[0]
+    for k in range(1, N_GROUP):
+        total = total + gather[k]
+    o_ref[la] = total
+
+    copies = []
+    for k in range(1, N_GROUP):
+        copy = pltpu.make_async_remote_copy(
+            src_ref=o_ref.at[la],
+            dst_ref=o_ref.at[la],
+            send_sem=s3.at[k],
+            recv_sem=r3.at[k],
+            device_id=lat_peer(k),
+            device_id_type=MESH,
+        )
+        copy.start()
+        copies.append(copy)
+    for copy in copies:
+        copy.wait()
+
+
+def reduce_all(parts):
+    flat = jnp.concatenate([p.reshape(-1) for p in parts])
+    room = N_GROUP * CHUNK * 128
+    block = jnp.pad(flat, (0, room - flat.shape[0])).reshape(N_GROUP, CHUNK, 128)
+    shape = (N_GROUP, CHUNK, 128)
+    out = pl.pallas_call(
+        reduce_kernel,
+        out_shape=jax.ShapeDtypeStruct(shape, jnp.float32),
+        in_specs=[pl.BlockSpec(memory_space=pltpu.VMEM)],
+        out_specs=pl.BlockSpec(memory_space=pltpu.VMEM),
+        scratch_shapes=[pltpu.VMEM(shape, jnp.float32)] * 2
+        + [pltpu.SemaphoreType.DMA((N_GROUP,))] * 6,
+        compiler_params=pltpu.CompilerParams(collective_id=0, has_side_effects=True),
+    )(block)
+    flat = out.reshape(-1)
+    outs, at = [], 0
+    for p in parts:
+        outs.append(flat[at : at + p.size].reshape(p.shape))
+        at += p.size
+    return outs
 
 
 def body(
@@ -129,9 +227,8 @@
     dconv_ext = extend_back(dconv)
     tap_sum = kernel_sums(dconv, state_ext, n_rows, n_cols)
     bias_conv_sum = jnp.sum(dconv, axis=(1, 2))
-    totals = lax.psum(
-        (point[0], point[1], point[2], point[3], point[4], point[5], tap_sum, bias_conv_sum),
-        ("lat", "lon"),
+    totals = reduce_all(
+        (point[0], point[1], point[2], point[3], point[4], point[5], tap_sum, bias_conv_sum)
     )
     state_grad = (
         cotangent.astype(jnp.float32) + transpose_conv(dconv_ext, kernel, n_rows, n_cols)

time: 423 us -> 123 us (0.29)
  the two profiles are of different devices: /device:TPU:1 before, /device:TPU:5 now
where the time goes in v1:
time: 123 us
  other arithmetic  33.1 us (27%)
  waiting for transfers between devices  28.3 us (23%)
  Pallas kernels  23.9 us (19%)
  starting transfers between devices  23.8 us (19%)
  local copies, waits for them, and re-layouts  8.69 us (7%)
  matrix products  3.76 us (3%)
    pallas_call x1, Pallas kernels, reduce_all(): pl.pallas_call(reduce_kernel, out_shape=jax.ShapeDtypeStruct(shape, jnp.f...  23.9 us
    ppermute x4, waiting for transfers between devices, extended(): after = lax.ppermute(first, axis, down)  16.4 us
    ppermute x4, starting transfers between devices, extended(): after = lax.ppermute(first, axis, down)  15.7 us
    ppermute x4, waiting for transfers between devices, extended(): before = lax.ppermute(last, axis, up)  11.9 us
    reduce_sum x3, other arithmetic, kernel_sums(): jnp.sum(dconv * padded[:, row_tap:row_tap + n_rows, col_tap:col_tap + n_c...  10.7 us
    reduce_sum x1, other arithmetic, cell_terms(): center = conv_out - jnp.mean(conv_out, axis=0, keepdims=True)  9.52 us
    ppermute x4, starting transfers between devices, extended(): before = lax.ppermute(last, axis, up)  8.14 us
    convert_element_type x1, other arithmetic, body(): state_grad = (cotangent.astype(jnp.float32) + transpose_conv(dconv_ext, k...  8.07 us
  transfers between devices with their start and end apart: 8, of which 7 were waited for; matrix products, arithmetic and copies ran while one was open for 3% of the time, Pallas kernels for 0%

profile of v1, /device:TPU:5, one launch (start us, length us, event | category | flops | bytes accessed | tf_op | source)
XLA Modules:
  0.0 122.6 jit_solution(11186773399982281108)
XLA Ops:
  0.7 1.3 %fusion.87 = (bf16[64,3,270]{2,1,0:T(4,128)(2,1)S(1)}, bf16[64,3,270]{2,1,0:T(4,128)(2,1)S(1)}) fusion(bf16[64,8,270]{2,1,0:T(8,128)(2,1)} %param.10), kind=kLoop, calls=%fused_computation.272 | loop fusion | bytes 414720 | tf_op jit(solution)/shard_map/slice | solution.py:24
  2.1 3.4 %collective-permute-start = (bf16[64,3,270]{2,0,1:T(8,128)(2,1)S(1)}, bf16[64,3,270]{2,0,1:T(8,128)(2,1)S(1)}, u32[]{:S(2)}, u32[]{:S(2)}) collective-permute-start(bf16[64,3,270]{2,0,1:T(8,128)(2,1)S(1)} %copy.47), channel_id=1, source_target_pairs={{0,16},{16,32},{32,48},{48,64},{64,80},{80,96},{96,112},{112,128},... | collective-permute-start | bytes 311048 | tf_op jit(solution)/shard_map/ppermute | solution.py:25
  5.5 1.9 %collective-permute-start.1 = (bf16[64,3,270]{2,0,1:T(8,128)(2,1)S(1)}, bf16[64,3,270]{2,0,1:T(8,128)(2,1)S(1)}, u32[]{:S(2)}, u32[]{:S(2)}) collective-permute-start(bf16[64,3,270]{2,0,1:T(8,128)(2,1)S(1)} %copy.48), channel_id=1, source_target_pairs={{16,0},{32,16},{48,32},{64,48},{80,64},{96,80},{112,96},{128,112},... | collective-permute-start | bytes 311048 | tf_op jit(solution)/shard_map/ppermute | solution.py:26
  8.2 3.8 %collective-permute-done.1 = bf16[64,3,270]{2,0,1:T(8,128)(2,1)S(1)} collective-permute-done((bf16[64,3,270]{2,0,1:T(8,128)(2,1)S(1)}, bf16[64,3,270]{2,0,1:T(8,128)(2,1)S(1)}, u32[]{:S(2)}, u32[]{:S(2)}) %collective-permute-start.1) | collective-permute-done | bytes 103712 | tf_op jit(solution)/shard_map/ppermute | solution.py:26
  12.1 1.7 %collective-permute-start.2 = (bf16[64,14,3]{2,0,1:T(8,128)(2,1)S(1)}, bf16[64,14,3]{2,0,1:T(8,128)(2,1)S(1)}, u32[]{:S(2)}, u32[]{:S(2)}) collective-permute-start(bf16[64,14,3]{2,0,1:T(8,128)(2,1)S(1)} %get-tuple-element.91), channel_id=1, source_target_pairs={{0,1},{1,2},{2,3},{3,4},{4,5},{5,6},{6,7},{7,8},{8,9},{9,10},{10,1... | collective-permute-start | bytes 16136 | tf_op jit(solution)/shard_map/ppermute | solution.py:25
  13.8 6.8 %collective-permute-start.3 = (bf16[64,14,3]{2,0,1:T(8,128)(2,1)S(1)}, bf16[64,14,3]{2,0,1:T(8,128)(2,1)S(1)}, u32[]{:S(2)}, u32[]{:S(2)}) collective-permute-start(bf16[64,14,3]{2,0,1:T(8,128)(2,1)S(1)} %get-tuple-element.92), channel_id=1, source_target_pairs={{1,0},{2,1},{3,2},{4,3},{5,4},{6,5},{7,6},{8,7},{9,8},{10,9},{11,1... | collective-permute-start | bytes 16136 | tf_op jit(solution)/shard_map/ppermute | solution.py:26
  20.7 4.8 %collective-permute-done.2 = bf16[64,14,3]{2,0,1:T(8,128)(2,1)S(1)} collective-permute-done((bf16[64,14,3]{2,0,1:T(8,128)(2,1)S(1)}, bf16[64,14,3]{2,0,1:T(8,128)(2,1)S(1)}, u32[]{:S(2)}, u32[]{:S(2)}) %collective-permute-start.2) | collective-permute-done | bytes 5408 | tf_op jit(solution)/shard_map/ppermute | solution.py:25
  26.1 9.5 %fusion.84 = (f32[8,270]{1,0:T(8,128)S(1)}, f32[64,8,270]{2,0,1:T(8,128)S(1)}) fusion(f32[64]{0:T(128)S(1)} %copy-done.7, f32[64,14,276]{2,0,1:T(8,128)S(1)} %maximum_convert_fusion, f32[64]{0:T(128)S(1)} %get-tuple-element.146, f32[64]{0:T(128)S(1)} %get-tuple-element.147, f32[64]{0:T(128)S(1)} %get-tuple-element.100, f32[64]{0:T(128)S(1)} %get-tuple-element.101, ...), kind=kLoop, calls=%fused_computation.269 | loop fusion | flops 13683600 | bytes 27669440 | tf_op jit(solution)/shard_map/reduce_sum | solution.py:90
  36.5 0.7 convolution_bitcast_fusion
  37.2 1.4 %convert_reduce_fusion = (f32[256]{0:T(256)S(1)}, bf16[256,8,270]{0,2,1:T(8,128)(2,1)S(1)}) fusion(f32[8,270,256]{2,1,0:T(8,128)S(1)} %fusion.79, f32[256]{0:T(256)S(1)} %copy-done.9, bf16[256,64]{0,1:T(8,128)(2,1)S(1)} %copy-done.8, bf16[64,8,270]{2,1,0:T(8,128)(2,1)S(1)} %get-tuple-element.82), kind=kOutput, calls=%fused_computation.13 | convolution fusion | flops 77967104 | bytes 3629056 | tf_op jit(solution)/shard_map/chw,ec->ehw/dot_general | solution.py:99
  39.0 0.7 fusion.72
  39.7 4.0 %multiply_reduce_fusion = (f32[64]{0:T(128)S(1)}, f32[64]{0:T(128)S(1)}, f32[64]{0:T(128)S(1)}, f32[64]{0:T(128)S(1)}, f32[64]{0:T(128)S(1)}, /*index=5*/f32[64]...) fusion(f32[64,14,276]{2,0,1:T(8,128)S(1)} %maximum_convert_fusi, ...), kind=kLoop, calls=%fused_computation.134 | loop fusion | flops 5943168 | bytes 11651584 | tf_op jit(solution)/shard_map/reduce_sum | solution.py:81
  43.7 2.7 %multiply_reduce_fusion.36 = (f32[64]{0:T(128)S(1)}, f32[64]{0:T(128)S(1)}, f32[64]{0:T(128)S(1)}, f32[64]{0:T(128)S(1)}, f32[64]{0:T(128)S(1)}, /*index=5*/f32[...) fusion(f32[64,8,270]{2,0,1:T(8,128)S(1)} %get-tuple-element.80,, ...), kind=kLoop, calls=%fused_computation.170 | loop fusion | flops 3731584 | bytes 7745024 | tf_op jit(solution)/shard_map/reduce_sum | solution.py:81
  46.4 4.0 %multiply_reduce_fusion.18 = (f32[64]{0:T(128)S(1)}, f32[64]{0:T(128)S(1)}, f32[64]{0:T(128)S(1)}, f32[64]{0:T(128)S(1)}, f32[64]{0:T(128)S(1)}, /*index=5*/f32[...) fusion(f32[64,8,270]{2,0,1:T(8,128)S(1)} %get-tuple-element.80,, ...), kind=kLoop, calls=%fused_computation.152 | loop fusion | flops 4975488 | bytes 10510848 | tf_op jit(solution)/shard_map/reduce_sum | solution.py:81
  51.2 0.7 reshape.67.x_ref
  51.9 23.9 %shard_map.169 = f32[16,18,128]{2,1,0:T(8,128)} custom-call(f32[16,18,128]{2,1,0:T(8,128)} %reshape.67.x_ref), custom_call_target="tpu_custom_call" | custom-call | tf_op jit(solution)/shard_map/pallas_call | solution.py:200
  75.8 0.9 reshape.68
  76.7 1.0 slice.796
  77.7 1.0 slice.799
  78.9 0.6 slice_multiply_fusion.43
  79.5 3.0 %collective-permute-start.4 = (f32[64,3,270]{2,0,1:T(8,128)S(1)}, f32[64,3,270]{2,0,1:T(8,128)S(1)}, u32[]{:S(2)}, u32[]{:S(2)}) collective-permute-start(f32[64,3,270]{2,0,1:T(8,128)S(1)} %get-tuple-element.89), channel_id=1, source_target_pairs={{0,16},{16,32},{32,48},{48,64},{64,80},{80,96},{96,112},{112,128},... | collective-permute-start | bytes 622088 | tf_op jit(solution)/shard_map/ppermute | solution.py:25
  82.6 1.9 %collective-permute-start.5 = (f32[64,3,270]{2,0,1:T(8,128)S(1)}, f32[64,3,270]{2,0,1:T(8,128)S(1)}, u32[]{:S(2)}, u32[]{:S(2)}) collective-permute-start(f32[64,3,270]{2,0,1:T(8,128)S(1)} %get-tuple-element.90), channel_id=1, source_target_pairs={{16,0},{32,16},{48,32},{64,48},{80,64},{96,80},{112,96},{128,112},... | collective-permute-start | bytes 622088 | tf_op jit(solution)/shard_map/ppermute | solution.py:26
  85.1 1.1 collective-permute-done.4
  86.2 4.4 %collective-permute-done.5 = f32[64,3,270]{2,0,1:T(8,128)S(1)} collective-permute-done((f32[64,3,270]{2,0,1:T(8,128)S(1)}, f32[64,3,270]{2,0,1:T(8,128)S(1)}, u32[]{:S(2)}, u32[]{:S(2)}) %collective-permute-start.5) | collective-permute-done | bytes 207392 | tf_op jit(solution)/shard_map/ppermute | solution.py:26
  90.6 1.1 pad_maximum_fusion.5
  91.7 5.0 %collective-permute-start.6 = (f32[64,14,3]{2,0,1:T(8,128)}, f32[64,14,3]{2,0,1:T(8,128)S(1)}, u32[]{:S(2)}, u32[]{:S(2)}) collective-permute-start(f32[64,14,3]{2,0,1:T(8,128)} %get-tuple-element.87), channel_id=1, source_target_pairs={{1,0},{2,1},{3,2},{4,3},{5,4},{6,5},{7,6},{8,7},{9,8},{10,9},{11,1... | collective-permute-start | bytes 32264 | tf_op jit(solution)/shard_map/ppermute | solution.py:26
  97.2 0.7 copy.37
  98.1 0.7 copy.36
  98.9 8.1 %collective-permute-done.6 = f32[64,14,3]{2,0,1:T(8,128)S(1)} collective-permute-done((f32[64,14,3]{2,0,1:T(8,128)}, f32[64,14,3]{2,0,1:T(8,128)S(1)}, u32[]{:S(2)}, u32[]{:S(2)}) %collective-permute-start.6) | collective-permute-done | bytes 10784 | tf_op jit(solution)/shard_map/ppermute | solution.py:26
  107.0 6.0 %collective-permute-done.7 = f32[64,14,3]{2,0,1:T(8,128)S(1)} collective-permute-done((f32[64,14,3]{2,0,1:T(8,128)}, f32[64,14,3]{2,0,1:T(8,128)S(1)}, u32[]{:S(2)}, u32[]{:S(2)}) %collective-permute-start.7) | collective-permute-done | bytes 10784 | tf_op jit(solution)/shard_map/ppermute | solution.py:25
  113.6 8.1 %fusion.73 = bf16[64,8,270]{2,0,1:T(8,128)(2,1)S(1)} fusion(f32[64,14,273]{2,0,1:T(8,128)S(1)} %get-tuple-element.86, f32[64,8,270]{2,0,1:T(8,128)S(1)} %get-tuple-element.80, f32[64,3,270]{2,0,1:T(8,128)S(1)} %collective-permute-done.4, f32[64,14,273]{2,0,1:T(8,128)S(1)} %get-tuple-element.85, f32[64,3,270]{2,0,1:T(8,128)S(1)} %collective-permute-done.5, ...), kind=kLoop, calls=%fused_computation.189 | loop fusion | flops 14653440 | bytes 24757504 | tf_op jit(solution)/shard_map/convert_element_type | solution.py:235
  121.7 1.0 copy.35
  (56 shorter events, 5.5 us)
Async XLA Ops:
  0.6 35.1 %copy-start = (bf16[64,256]{1,0:T(8,128)(2,1)S(1)}, bf16[64,256]{1,0:T(8,128)(2,1)}, u32[]{:S(2)}) copy-start(bf16[64,256]{1,0:T(8,128)(2,1)} %param.17) | copy-start | bytes 98308
  0.7 7.4 %copy-start.2 = (bf16[64,8,270]{2,1,0:T(8,128)(2,1)S(1)}, bf16[64,8,270]{2,1,0:T(8,128)(2,1)}, u32[]{:S(2)}) copy-start(bf16[64,8,270]{2,1,0:T(8,128)(2,1)} %param.10) | copy-start | bytes 829444
  0.7 6.8 %copy-start.4 = (s32[8,270]{1,0:T(8,128)S(1)}, s32[8,270]{1,0:T(8,128)}, u32[]{:S(2)}) copy-start(s32[8,270]{1,0:T(8,128)} %param.11) | copy-start | bytes 25924
  0.7 6.8 %copy-start.3 = (f32[64,7,7]{0,2,1:T(8,128)S(1)}, f32[64,7,7]{0,2,1:T(8,128)}, u32[]{:S(2)}) copy-start(f32[64,7,7]{0,2,1:T(8,128)} %param.13) | copy-start | bytes 37636
  0.7 6.8 %copy-start.1 = (bf16[64,8,270]{2,1,0:T(8,128)(2,1)S(1)}, bf16[64,8,270]{2,1,0:T(8,128)(2,1)}, u32[]{:S(2)}) copy-start(bf16[64,8,270]{2,1,0:T(8,128)(2,1)} %param.12) | copy-start | bytes 829444
  2.1 6.0 %collective-permute-start = (bf16[64,3,270]{2,0,1:T(8,128)(2,1)S(1)}, bf16[64,3,270]{2,0,1:T(8,128)(2,1)S(1)}, u32[]{:S(2)}, u32[]{:S(2)}) collective-permute-start(bf16[64,3,270]{2,0,1:T(8,128)(2,1)S(1)} %copy.47), channel_id=1, source_target_pairs={{0,16},{16,32},{32,48},{48,64},{64,80},{80,96},{96,112},{112,128},... | collective-permute-start | bytes 311048 | tf_op jit(solution)/shard_map/ppermute | solution.py:25
  5.5 6.5 %collective-permute-start.1 = (bf16[64,3,270]{2,0,1:T(8,128)(2,1)S(1)}, bf16[64,3,270]{2,0,1:T(8,128)(2,1)S(1)}, u32[]{:S(2)}, u32[]{:S(2)}) collective-permute-start(bf16[64,3,270]{2,0,1:T(8,128)(2,1)S(1)} %copy.48), channel_id=1, source_target_pairs={{16,0},{32,16},{48,32},{64,48},{80,64},{96,80},{112,96},{128,112},... | collective-permute-start | bytes 311048 | tf_op jit(solution)/shard_map/ppermute | solution.py:26
  12.1 13.9 %copy-start.7 = (f32[64]{0:T(128)S(1)}, f32[64]{0:T(128)}, u32[]{:S(2)}) copy-start(f32[64]{0:T(128)} %param.14) | copy-start | bytes 772
  12.1 13.4 %collective-permute-start.2 = (bf16[64,14,3]{2,0,1:T(8,128)(2,1)S(1)}, bf16[64,14,3]{2,0,1:T(8,128)(2,1)S(1)}, u32[]{:S(2)}, u32[]{:S(2)}) collective-permute-start(bf16[64,14,3]{2,0,1:T(8,128)(2,1)S(1)} %get-tuple-element.91), channel_id=1, source_target_pairs={{0,1},{1,2},{2,3},{3,4},{4,5},{5,6},{6,7},{7,8},{8,9},{9,10},{10,1... | collective-permute-start | bytes 16136 | tf_op jit(solution)/shard_map/ppermute | solution.py:25
  13.8 11.8 %collective-permute-start.3 = (bf16[64,14,3]{2,0,1:T(8,128)(2,1)S(1)}, bf16[64,14,3]{2,0,1:T(8,128)(2,1)S(1)}, u32[]{:S(2)}, u32[]{:S(2)}) collective-permute-start(bf16[64,14,3]{2,0,1:T(8,128)(2,1)S(1)} %get-tuple-element.92), channel_id=1, source_target_pairs={{1,0},{2,1},{3,2},{4,3},{5,4},{6,5},{7,6},{8,7},{9,8},{10,9},{11,1... | collective-permute-start | bytes 16136 | tf_op jit(solution)/shard_map/ppermute | solution.py:26
  26.0 9.7 %copy-start.5 = (f32[64]{0:T(128)S(1)}, f32[64]{0:T(128)}, u32[]{:S(2)}) copy-start(f32[64]{0:T(128)} %param.15) | copy-start | bytes 772
  26.1 9.7 %copy-start.6 = (f32[64]{0:T(128)S(1)}, f32[64]{0:T(128)}, u32[]{:S(2)}) copy-start(f32[64]{0:T(128)} %param.16) | copy-start | bytes 772
  35.8 0.7 copy-start.9
  36.5 0.8 copy-start.8
  79.5 6.7 %collective-permute-start.4 = (f32[64,3,270]{2,0,1:T(8,128)S(1)}, f32[64,3,270]{2,0,1:T(8,128)S(1)}, u32[]{:S(2)}, u32[]{:S(2)}) collective-permute-start(f32[64,3,270]{2,0,1:T(8,128)S(1)} %get-tuple-element.89), channel_id=1, source_target_pairs={{0,16},{16,32},{32,48},{48,64},{64,80},{80,96},{96,112},{112,128},... | collective-permute-start | bytes 622088 | tf_op jit(solution)/shard_map/ppermute | solution.py:25
  82.6 8.0 %collective-permute-start.5 = (f32[64,3,270]{2,0,1:T(8,128)S(1)}, f32[64,3,270]{2,0,1:T(8,128)S(1)}, u32[]{:S(2)}, u32[]{:S(2)}) collective-permute-start(f32[64,3,270]{2,0,1:T(8,128)S(1)} %get-tuple-element.90), channel_id=1, source_target_pairs={{16,0},{32,16},{48,32},{64,48},{80,64},{96,80},{112,96},{128,112},... | collective-permute-start | bytes 622088 | tf_op jit(solution)/shard_map/ppermute | solution.py:26
  91.7 15.4 %collective-permute-start.6 = (f32[64,14,3]{2,0,1:T(8,128)}, f32[64,14,3]{2,0,1:T(8,128)S(1)}, u32[]{:S(2)}, u32[]{:S(2)}) collective-permute-start(f32[64,14,3]{2,0,1:T(8,128)} %get-tuple-element.87), channel_id=1, source_target_pairs={{1,0},{2,1},{3,2},{4,3},{5,4},{6,5},{7,6},{8,7},{9,8},{10,9},{11,1... | collective-permute-start | bytes 32264 | tf_op jit(solution)/shard_map/ppermute | solution.py:26
  96.7 16.3 %collective-permute-start.7 = (f32[64,14,3]{2,0,1:T(8,128)}, f32[64,14,3]{2,0,1:T(8,128)S(1)}, u32[]{:S(2)}, u32[]{:S(2)}) collective-permute-start(f32[64,14,3]{2,0,1:T(8,128)} %get-tuple-element.88), channel_id=1, source_target_pairs={{0,1},{1,2},{2,3},{3,4},{4,5},{5,6},{6,7},{7,8},{8,9},{9,10},{10,1... | collective-permute-start | bytes 32264 | tf_op jit(solution)/shard_map/ppermute | solution.py:25

commit v2 on v1

v2 whole, which is shorter than its diff:
```python
import math

import jax
import jax.numpy as jnp
from jax import lax
from jax.experimental import pallas as pl
from jax.experimental.pallas import tpu as pltpu
from jax.sharding import PartitionSpec as P

TAPS = 7
CHAN = 64
EXPAND = 256
ROWS = 8
COLS = 270
HALF = 135
PITCH = 136
TILES = 17
CELLS = ROWS * PITCH
EXT_ROWS = 14
EXT_COLS = 144
STEP = 272
N_GROUP = 16
CHUNK = 18
MESH = pl.DeviceIdType.MESH

ln_eps = 1e-06
root_half = 0.7071067811865476
inv_root_tau = 0.3989422804014327

f32 = jnp.float32
bf16 = jnp.bfloat16


def dot(a, b, dims):
    return lax.dot_general(a, b, (dims, ((), ())), preferred_element_type=f32)


NN = ((1,), (0,))
NT = ((1,), (1,))
TN = ((0,), (0,))


def split(x):
    hi = x.astype(bf16)
    lo = (x - hi.astype(f32)).astype(bf16)
    return jnp.concatenate([hi, lo], axis=1)


def kernel_body(
    state_hbm,
    cot_hbm,
    land_ref,
    prm_ref,
    be_ref,
    we_ref,
    wp_ref,
    grad_ref,
    expand_ref,
    project_ref,
    small_ref,
    state_in,
    cot_in,
    planes,
    turned,
    s_ext,
    d_ext,
    wet32,
    wet16,
    x_ref,
    norm_ref,
    rstd_ref,
    zed_ref,
    pre_ref,
    dact_ref,
    act_ref,
    dhid_ref,
    taps_ref,
    wbd,
    wpbd,
    mean_ref,
    eg_ref,
    pg_ref,
    acc_ref,
    tap_out,
    pay,
    part,
    gather,
    total_ref,
    row_send,
    row_recv,
    col_send,
    col_recv,
    in_sem,
    row_ssem,
    row_rsem,
    col_ssem,
    col_rsem,
    s1,
    r1,
    s2,
    r2,
    s3,
    r3,
):
    la = lax.axis_index("lat")
    lo = lax.axis_index("lon")
    east = lax.rem(lo + 1, N_GROUP)
    west = lax.rem(lo + N_GROUP - 1, N_GROUP)
    has_north = la > 0
    has_south = la < N_GROUP - 1

    state_copy = pltpu.make_async_copy(state_hbm, state_in, in_sem.at[0])
    state_copy.start()
    cot_copy = pltpu.make_async_copy(cot_hbm, cot_in, in_sem.at[1])
    cot_copy.start()

    def lat_peer(k):
        return {"lat": lax.rem(la + k, N_GROUP), "lon": lo}

    def lon_peer(k):
        return {"lat": la, "lon": lax.rem(lo + k, N_GROUP)}

    barrier = pltpu.get_barrier_semaphore()
    for k in range(1, N_GROUP):
        pl.semaphore_signal(barrier, inc=1, device_id=lat_peer(k), device_id_type=MESH)
        pl.semaphore_signal(barrier, inc=1, device_id=lon_peer(k), device_id_type=MESH)
    for side in (east, west):

        @pl.when(has_north)
        def _():
            pl.semaphore_signal(
                barrier, inc=1, device_id={"lat": la - 1, "lon": side}, device_id_type=MESH
            )

        @pl.when(has_south)
        def _():
            pl.semaphore_signal(
                barrier, inc=1, device_id={"lat": la + 1, "lon": side}, device_id_type=MESH
            )

    lane = lax.broadcasted_iota(jnp.int32, (ROWS, 8, 128), 2)
    sub = lax.broadcasted_iota(jnp.int32, (ROWS, 8, 128), 1)

    for i in range(TAPS * TAPS):
        taps_ref[i] = jnp.broadcast_to(prm_ref[i : i + 1, :], (8, 128))
    wbd[...] = jnp.zeros((128, 512), bf16)
    wbd[0:64, 0:256] = we_ref[...]
    wbd[64:128, 256:512] = we_ref[...]
    nothing = jnp.zeros((EXPAND, CHAN), bf16)
    wpbd[0:256, :] = jnp.concatenate([wp_ref[...], nothing], axis=1)
    wpbd[256:512, :] = jnp.concatenate([nothing, wp_ref[...]], axis=1)
    at_row = lax.broadcasted_iota(jnp.int32, (256, 128), 0)
    at_col = lax.broadcasted_iota(jnp.int32, (256, 128), 1)
    same = lax.rem(at_row, 128) // 64 == at_col // 64
    mean_ref[...] = jnp.where(same, 1.0 / CHAN, 0.0).astype(bf16)

    conv_bias = prm_ref[49:50, :]
    gain = prm_ref[50:51, :]
    ln_bias = prm_ref[51:52, :]

    s_ext[:, 136:144, :] = jnp.zeros((EXT_ROWS, 8, 128), f32)
    d_ext[:, 136:144, :] = jnp.zeros((EXT_ROWS, 8, 128), f32)
    for ref in (s_ext, d_ext):

        @pl.when(jnp.logical_not(has_north))
        def _():
            ref[0:3] = jnp.zeros((3, EXT_COLS, 128), f32)

        @pl.when(jnp.logical_not(has_south))
        def _():
            ref[11:14] = jnp.zeros((3, EXT_COLS, 128), f32)

    planes[2] = jnp.zeros((CHAN * ROWS, 128), f32)

    def to_planes(load):
        def step(i, carry):
            at = pl.ds(pl.multiple_of(i * 8, 8), 8)
            x = load(at)
            to = pl.ds(pl.multiple_of(i * 64, 64), 64)
            planes[0, to, :] = x[:, :, 0:128].reshape(64, 128)
            planes[1, to, :] = x[:, :, 128:256].reshape(64, 128)
            planes[2, to, 0:14] = x[:, :, 256:270].reshape(64, 14)
            return carry

        lax.fori_loop(0, 8, step, 0)

    half_lane = lax.broadcasted_iota(jnp.int32, (PITCH, 128), 1) < 64

    def turn_in(put):
        def step(p, carry):
            r = p * 2
            for k in range(3):
                both = jnp.concatenate(
                    [
                        planes[k, pl.ds(r, CHAN, stride=ROWS), :],
                        planes[k, pl.ds(r + 1, CHAN, stride=ROWS), :],
                    ],
                    axis=0,
                )
                turned[128 * k : 128 * k + 128, :] = both.T
            h0 = turned[0:PITCH, :]
            h1 = turned[HALF : HALF + PITCH, :]
            put(r, jnp.where(half_lane, h0, pltpu.roll(h1, 64, axis=1)))
            put(r + 1, jnp.where(half_lane, pltpu.roll(h0, 64, axis=1), h1))
            return carry

        lax.fori_loop(0, ROWS // 2, step, 0)

    def exchange(ext, n):
        to_east = pltpu.roll(ext[3:11, 135:143, :], 64, axis=2)
        to_west = pltpu.roll(ext[3:11, 1:9, :], 64, axis=2)
        col_send[n, 0] = to_east
        col_send[n, 1] = to_west
        ext[3:11, 0:8, :] = jnp.where((sub < 3) & (lane >= 64), to_east, ext[3:11, 0:8, :])
        ext[3:11, 136:144, :] = jnp.where(
            (sub >= 2) & (sub < 5) & (lane < 64), to_west, ext[3:11, 136:144, :]
        )
        row_send[n, 0] = ext[3:6].astype(bf16)
        row_send[n, 1] = ext[8:11].astype(bf16)

    def rows_copy(n, way):
        return pltpu.make_async_remote_copy(
            src_ref=row_send.at[n, way],
            dst_ref=row_recv.at[n, way],
            send_sem=row_ssem.at[n, way],
            recv_sem=row_rsem.at[n, way],
            device_id={"lat": la - 1 + 2 * way, "lon": lo},
            device_id_type=MESH,
        )

    def cols_copy(n, way, turn):
        src = col_send.at[n, way]
        dst = col_recv.at[n, way]
        if turn == 1:
            src, dst = src.at[0:3], dst.at[11:14]
        elif turn == 2:
            src, dst = src.at[5:8], dst.at[0:3]
        else:
            dst = dst.at[3:11]
        return pltpu.make_async_remote_copy(
            src_ref=src,
            dst_ref=dst,
            send_sem=col_ssem.at[n, way, turn],
            recv_sem=col_rsem.at[n, way, turn],
            device_id={
                "lat": la + (0, -1, 1)[turn],
                "lon": (east, west)[way],
            },
            device_id_type=MESH,
        )

    def start_copies(n):
        @pl.when(has_north)
        def _():
            rows_copy(n, 0).start()
            cols_copy(n, 0, 1).start()
            cols_copy(n, 1, 1).start()

        @pl.when(has_south)
        def _():
            rows_copy(n, 1).start()
            cols_copy(n, 0, 2).start()
            cols_copy(n, 1, 2).start()

        cols_copy(n, 0, 0).start()
        cols_copy(n, 1, 0).start()

    def finish_copies(ext, n):
        @pl.when(has_north)
        def _():
            rows_copy(n, 0).wait_send()
            cols_copy(n, 0, 1).wait_send()
            cols_copy(n, 1, 1).wait_send()
            rows_copy(n, 1).wait_recv()
            cols_copy(n, 0, 2).wait_recv()
            cols_copy(n, 1, 2).wait_recv()
            ext[0:3] = row_recv[n, 1].astype(f32)

        @pl.when(has_south)
        def _():
            rows_copy(n, 1).wait_send()
            cols_copy(n, 0, 2).wait_send()
            cols_copy(n, 1, 2).wait_send()
            rows_copy(n, 0).wait_recv()
            cols_copy(n, 0, 1).wait_recv()
            cols_copy(n, 1, 1).wait_recv()
            ext[11:14] = row_recv[n, 0].astype(f32)

        cols_copy(n, 0, 0).wait()
        cols_copy(n, 1, 0).wait()

        def fill(first, last):
            from_west = col_recv[n, 0, first:last]
            from_east = col_recv[n, 1, first:last]
            m = last - first
            ext[first:last, 0:8, :] = jnp.where(
                (sub[:m] < 3) & (lane[:m] < 64), from_west, ext[first:last, 0:8, :]
            )
            ext[first:last, 136:144, :] = jnp.where(
                (sub[:m] >= 2) & (sub[:m] < 5) & (lane[:m] >= 64),
                from_east,
                ext[first:last, 136:144, :],
            )

        fill(3, 11)

        @pl.when(has_north)
        def _():
            fill(0, 3)

        @pl.when(has_south)
        def _():
            fill(11, 14)

    def convolve(ext, flip, bias):
        def step(t, carry):
            at = pl.multiple_of(t * 8, 8)
            acc = jnp.zeros((ROWS, 8, 128), f32)
            if bias is not None:
                acc = acc + bias[None]
            for b in range(TAPS):
                x = ext[:, pl.ds(at + b, 8), :]
                for a in range(TAPS):
                    i = a * TAPS + b
                    acc = acc + taps_ref[48 - i if flip else i][None] * x[a : a + ROWS]
            for r in range(ROWS):
                x_ref[pl.ds(at + r * PITCH, 8), :] = acc[r]
            return carry

        lax.fori_loop(0, TILES, step, 0)

    state_copy.wait()
    to_planes(lambda at: state_in[at].astype(f32))

    def put_state(r, value):
        s_ext[r + 3, 3 : 3 + PITCH, :] = value

    turn_in(put_state)
    exchange(s_ext, 0)
    pl.semaphore_wait(
        barrier,
        2 * (N_GROUP - 1)
        + 2 * has_north.astype(jnp.int32)
        + 2 * has_south.astype(jnp.int32),
    )
    start_copies(0)

    cot_copy.wait()
    land = land_ref[...].astype(f32)
    to_planes(lambda at: cot_in[at].astype(f32) * land[None])

    def put_wet(r, value):
        wet32[pl.ds(pl.multiple_of(r * PITCH, 8), PITCH), :] = value
        wet32[pl.ds(r * PITCH + HALF, 1), :] = jnp.zeros((1, 128), f32)

    turn_in(put_wet)
    acc_ref[...] = jnp.zeros((5, 8, 512), f32)
    eg_ref[...] = jnp.zeros((128, 512), f32)
    pg_ref[...] = jnp.zeros((128, 512), f32)

    def narrow(i, carry):
        at = pl.ds(pl.multiple_of(i * 16, 16), 16)
        w = wet32[at, :]
        wet16[at, :] = w.astype(bf16)
        return carry + w[0:8] + w[8:16]

    acc_ref[0, :, 0:128] = lax.fori_loop(0, CELLS // 16, narrow, jnp.zeros((8, 128), f32))

    finish_copies(s_ext, 0)
    convolve(s_ext, False, conv_bias)

    def fold(x):
        return jnp.sum(x.reshape(-1, 8, x.shape[-1]), axis=0)

    def pointwise(q, carry):
        at = pl.ds(pl.multiple_of(q * STEP, STEP), STEP)
        x = x_ref[at, :]
        cen = x - dot(split(x), mean_ref[...], NN)
        rstd = lax.rsqrt(dot(split(cen * cen), mean_ref[...], NN) + ln_eps)
        normed = cen * rstd
        zed = (normed * gain + ln_bias).astype(bf16)
        norm_ref[...] = normed
        rstd_ref[...] = rstd
        zed_ref[...] = zed
        pre_ref[...] = dot(zed, wbd[...], NN)
        wet = wet16[at, :]
        dact_ref[...] = dot(wet, wpbd[...], NT)

        def gelu(i, total):
            rows = pl.ds(pl.multiple_of(i * 16, 16), 16)
            for k in range(4):
                cols = slice(128 * k, 128 * k + 128)
                pre = pre_ref[rows, cols] + be_ref[0:1, cols]
                grow = jnp.exp(-0.5 * pre * pre)
                t = 1.0 / (1.0 + (0.3275911 * root_half) * jnp.abs(pre))
                poly = 0.5 * 1.061405429 * t - 0.5 * 1.453152027
                poly = poly * t + 0.5 * 1.421413741
                poly = poly * t - 0.5 * 0.284496736
                poly = poly * t + 0.5 * 0.254829592
                tail = poly * t * grow
                phi = jnp.where(pre >= 0, 1.0 - tail, tail)
                slope = phi + pre * grow * inv_root_tau
                act_ref[rows, cols] = (pre * phi).astype(bf16)
                dhid = (dact_ref[rows, cols] * slope).astype(bf16)
                dhid_ref[rows, cols] = dhid
                wide = dhid.astype(f32)
                acc_ref[1, :, cols] += wide[0:8] + wide[8:16]
            return total

        lax.fori_loop(0, STEP // 16, gelu, 0)
        dhid = dhid_ref[...]
        dzed = dot(dhid, wbd[...], NT)
        normed = norm_ref[...]
        acc_ref[2, :, 0:128] += fold(dzed * normed)
        acc_ref[3, :, 0:128] += fold(dzed)
        dnorm = dzed * gain
        m1 = dot(split(dnorm), mean_ref[...], NN)
        m2 = dot(split(dnorm * normed), mean_ref[...], NN)
        dconv = rstd_ref[...] * (dnorm - m1 - normed * m2)
        x_ref[at, :] = dconv
        acc_ref[4, :, 0:128] += fold(dconv)
        eg_ref[...] += dot(zed_ref[...], dhid, TN)
        pg_ref[...] += dot(wet16[at, :], act_ref[...], TN)
        return carry

    lax.fori_loop(0, CELLS // STEP, pointwise, 0)

    def place(r, carry):
        d_ext[r + 3, 3 : 3 + PITCH, :] = x_ref[pl.ds(pl.multiple_of(r * PITCH, 8), PITCH), :]
        return carry

    lax.fori_loop(0, ROWS, place, 0)
    exchange(d_ext, 1)
    start_copies(1)

    for b in range(TAPS):

        def tap_step(t, acc):
            at = pl.multiple_of(t * 8, 8)
            x = s_ext[:, pl.ds(at + b, 8), :]
            d = [x_ref[pl.ds(at + r * PITCH, 8), :] for r in range(ROWS)]
            new = []
            for a in range(TAPS):
                s = acc[a]
                for r in range(ROWS):
                    s = s + d[r] * x[r + a]
                new.append(s)
            return tuple(new)

        zero = jnp.zeros((8, 128), f32)
        acc = lax.fori_loop(0, TILES, tap_step, (zero,) * TAPS)
        for a in range(TAPS):
            tap_out[a * TAPS + b] = acc[a]

    def halves(x):
        return x + pltpu.roll(x, 64, axis=1)

    first_half = lax.broadcasted_iota(jnp.int32, (1, 128), 1) < 64
    for i in range(N_GROUP):
        c, e = 8 * (i // 2), 128 * (i % 2)
        pay[i, 0:8, :] = (
            eg_ref[c : c + 8, e : e + 128] + eg_ref[64 + c : 72 + c, 256 + e : 384 + e]
        )
        pay[i, 8:16, :] = (
            pg_ref[c : c + 8, e : e + 128] + pg_ref[64 + c : 72 + c, 256 + e : 384 + e]
        )

    def sums_of(x):
        return halves(jnp.sum(x, axis=0, keepdims=True))

    rows = []
    for i in range(25):
        one = sums_of(tap_out[i])
        two = sums_of(tap_out[25 + i]) if i < 24 else jnp.zeros((1, 128), f32)
        rows.append(jnp.where(first_half, one, two))
    wide = jnp.sum(acc_ref[1], axis=0, keepdims=True)
    wide = wide[:, 0:256] + wide[:, 256:512]
    rows.append(wide[:, 0:128])
    rows.append(wide[:, 128:256])
    rows.append(
        jnp.where(first_half, sums_of(acc_ref[4, :, 0:128]), sums_of(acc_ref[2, :, 0:128]))
    )
    rows.append(
        jnp.where(first_half, sums_of(acc_ref[3, :, 0:128]), sums_of(acc_ref[0, :, 0:128]))
    )
    while len(rows) < 32:
        rows.append(jnp.zeros((1, 128), f32))
    for i in range(N_GROUP):
        pay[i, 16:17, :] = rows[2 * i]
        pay[i, 17:18, :] = rows[2 * i + 1]

    copies1 = []
    for k in range(1, N_GROUP):
        copy = pltpu.make_async_remote_copy(
            src_ref=pay.at[lax.rem(la + k, N_GROUP)],
            dst_ref=part.at[k],
            send_sem=s1.at[k],
            recv_sem=r1.at[k],
            device_id=lat_peer(k),
            device_id_type=MESH,
        )
        copy.start()
        copies1.append(copy)

    finish_copies(d_ext, 1)
    convolve(d_ext, True, None)

    total = pay[la]
    for k in range(1, N_GROUP):
        copies1[k - 1].wait()
        total = total + part[k]
    gather[lo] = total
    copies2 = []
    for k in range(1, N_GROUP):
        copy = pltpu.make_async_remote_copy(
            src_ref=gather.at[lo],
            dst_ref=gather.at[lo],
            send_sem=s2.at[k],
            recv_sem=r2.at[k],
            device_id=lon_peer(k),
            device_id_type=MESH,
        )
        copy.start()
        copies2.append(copy)

    def turn_out(p, carry):
        r = p * 2
        g0 = x_ref[pl.ds(pl.multiple_of(r * PITCH, 8), PITCH), :]
        g1 = x_ref[pl.ds(pl.multiple_of(r * PITCH + PITCH, 8), PITCH), :]
        turned[0:PITCH, :] = jnp.where(half_lane, g0, pltpu.roll(g1, 64, axis=1))
        turned[HALF : HALF + PITCH, :] = jnp.where(half_lane, pltpu.roll(g0, 64, axis=1), g1)
        for k in range(3):
            back = turned[128 * k : 128 * k + 128, :].T
            planes[k, pl.ds(r, CHAN, stride=ROWS), :] = back[0:64]
            planes[k, pl.ds(r + 1, CHAN, stride=ROWS), :] = back[64:128]
        return carry

    lax.fori_loop(0, ROWS // 2, turn_out, 0)

    def write_out(i, carry):
        at = pl.ds(pl.multiple_of(i * 8, 8), 8)
        of = pl.ds(pl.multiple_of(i * 64, 64), 64)
        for k in range(3):
            cols = slice(128 * k, min(128 * k + 128, COLS))
            width = cols.stop - cols.start
            value = planes[k, of, 0:width].reshape(8, 8, width)
            grad_ref[at, :, cols] = (cot_in[at, :, cols].astype(f32) + value).astype(bf16)
        return carry

    lax.fori_loop(0, 8, write_out, 0)

    for copy in copies2:
        copy.wait()
    total = gather[0]
    for k in range(1, N_GROUP):
        total = total + gather[k]
    scale = 1.0 / math.sqrt(ROWS * N_GROUP * COLS * N_GROUP)
    total_ref[la] = total * scale
    copies3 = []
    for k in range(1, N_GROUP):
        copy = pltpu.make_async_remote_copy(
            src_ref=total_ref.at[la],
            dst_ref=total_ref.at[la],
            send_sem=s3.at[k],
            recv_sem=r3.at[k],
            device_id=lat_peer(k),
            device_id_type=MESH,
        )
        copy.start()
        copies3.append(copy)
    for copy in copies3:
        copy.wait()

    for e in range(2):
        pieces = []
        for c in range(8):
            i = 2 * c + e
            expand_ref[8 * c : 8 * c + 8, 128 * e : 128 * e + 128] = total_ref[i, 0:8, :]
            pieces.append(total_ref[i, 8:16, :])
        pieces.append(jnp.zeros((64, 128), f32))
        project_ref[128 * e : 128 * e + 128, :] = jnp.concatenate(pieces, axis=0).T[:, 0:64]
    for i in range(N_GROUP):
        small_ref[2 * i : 2 * i + 2, :] = total_ref[i, 16:18, :]


def body(
    state, land_sea, cotangent, kernel, conv_bias, ln_gain, ln_bias, w_expand, b_expand, w_project
):
    taps = kernel.reshape(CHAN, TAPS * TAPS).T
    prm = jnp.concatenate(
        [taps, conv_bias[None], ln_gain[None], ln_bias[None], jnp.zeros((4, CHAN), f32)], axis=0
    )
    prm = jnp.concatenate([prm, prm], axis=1)
    be = jnp.concatenate([b_expand, b_expand])[None]
    vmem = pl.BlockSpec(memory_space=pltpu.VMEM)
    anyw = pl.BlockSpec(memory_space=pl.ANY)
    sds = jax.ShapeDtypeStruct
    sem = pltpu.SemaphoreType.DMA
    piece = (N_GROUP, CHUNK, 128)
    grad, expand, project, small = pl.pallas_call(
        kernel_body,
        out_shape=(
            sds((CHAN, ROWS, COLS), bf16),
            sds((CHAN, EXPAND), f32),
            sds((EXPAND, CHAN), f32),
            sds((32, 128), f32),
        ),
        in_specs=[anyw, anyw, vmem, vmem, vmem, vmem, vmem],
        out_specs=(vmem, vmem, vmem, vmem),
        scratch_shapes=[
            pltpu.VMEM((CHAN, ROWS, COLS), bf16),
            pltpu.VMEM((CHAN, ROWS, COLS), bf16),
            pltpu.VMEM((3, CHAN * ROWS, 128), f32),
            pltpu.VMEM((384, 128), f32),
            pltpu.VMEM((EXT_ROWS, EXT_COLS, 128), f32),
            pltpu.VMEM((EXT_ROWS, EXT_COLS, 128), f32),
            pltpu.VMEM((CELLS, 128), f32),
            pltpu.VMEM((CELLS, 128), bf16),
            pltpu.VMEM((CELLS, 128), f32),
            pltpu.VMEM((STEP, 128), f32),
            pltpu.VMEM((STEP, 128), f32),
            pltpu.VMEM((STEP, 128), bf16),
            pltpu.VMEM((STEP, 512), f32),
            pltpu.VMEM((STEP, 512), f32),
            pltpu.VMEM((STEP, 512), bf16),
            pltpu.VMEM((STEP, 512), bf16),
            pltpu.VMEM((TAPS * TAPS, 8, 128), f32),
            pltpu.VMEM((128, 512), bf16),
            pltpu.VMEM((512, 128), bf16),
            pltpu.VMEM((256, 128), bf16),
            pltpu.VMEM((128, 512), f32),
            pltpu.VMEM((128, 512), f32),
            pltpu.VMEM((5, 8, 512), f32),
            pltpu.VMEM((TAPS * TAPS, 8, 128), f32),
            pltpu.VMEM(piece, f32),
            pltpu.VMEM(piece, f32),
            pltpu.VMEM(piece, f32),
            pltpu.VMEM(piece, f32),
            pltpu.VMEM((2, 2, 3, EXT_COLS, 128), bf16),
            pltpu.VMEM((2, 2, 3, EXT_COLS, 128), bf16),
            pltpu.VMEM((2, 2, ROWS, 8, 128), f32),
            pltpu.VMEM((2, 2, EXT_ROWS, 8, 128), f32),
            sem((2,)),
            sem((2, 2)),
            sem((2, 2)),
            sem((2, 2, 3)),
            sem((2, 2, 3)),
            sem((N_GROUP,)),
            sem((N_GROUP,)),
            sem((N_GROUP,)),
            sem((N_GROUP,)),
            sem((N_GROUP,)),
            sem((N_GROUP,)),
        ],
        compiler_params=pltpu.CompilerParams(
            collective_id=0, has_side_effects=True, vmem_limit_bytes=48 * 2**20
        ),
    )(state, cotangent, land_sea, prm, be, w_expand, w_project)
    tap_rows = jnp.concatenate([small[0:25, 0:64], small[0:24, 64:128]], axis=0)
    kernel_grad = tap_rows.T.reshape(CHAN, TAPS, TAPS)
    return (
        grad,
        kernel_grad,
        small[27, 0:64],
        small[27, 64:128],
        small[28, 0:64],
        expand,
        small[25:27].reshape(EXPAND),
        project,
        small[28, 64:128],
    )


def solution(mesh):
    in_specs = (
        P(None, "lat", "lon"),
        P("lat", "lon"),
        P(None, "lat", "lon"),
        P(),
        P(),
        P(),
        P(),
        P(),
        P(),
        P(),
    )
    out_specs = (P(None, "lat", "lon"), P(), P(), P(), P(), P(), P(), P(), P())
    return jax.shard_map(body, mesh=mesh, in_specs=in_specs, out_specs=out_specs, check_vma=False)
```

time: 123 us -> 56.6 us (0.46)
  the two profiles are of different devices: /device:TPU:5 before, /device:TPU:1 now
where the time goes in v2:
time: 56.6 us; the launch traced here: 56.2 us
  Pallas kernels  46 us (81%)
  local copies, waits for them, and re-layouts  9.47 us (17%)
  between operations  0.69 us (1%)
    pallas_call x1, Pallas kernels, body(): pl.pallas_call(kernel_body, out_shape=(sds((CHAN, ROWS, COLS), bf16), sds...  46 us
    unnamed x22, local copies, waits for them, and re-layouts  6.85 us

profile of v2, /device:TPU:1, one launch (start us, length us, event | category | flops | bytes accessed | tf_op | source)
XLA Modules:
  0.0 56.2 jit_solution(9926021483730613195)
XLA Ops:
  0.6 0.0 copy-start.5
  0.7 0.7 %copy-done.5 = f32[256]{0:T(256)S(1)} copy-done((f32[256]{0:T(256)S(1)}, f32[256]{0:T(256)}, u32[]{:S(2)}) %copy-start.5) | copy-done | bytes 1048
  1.3 0.8 %reshape.27 = f32[64,49]{0,1:T(8,128)S(1)} reshape(f32[64,7,7]{0,2,1:T(8,128)} %param.13) | data formatting | bytes 25088 | tf_op jit(solution)/shard_map/reshape | solution.py:589
  2.1 0.0 copy-start.6
  2.1 0.0 copy-start.7
  2.1 0.0 copy-start.8
  2.1 0.6 %copy-done.6 = f32[64]{0:T(128)S(1)} copy-done((f32[64]{0:T(128)S(1)}, f32[64]{0:T(128)}, u32[]{:S(2)}) %copy-start.6) | copy-done | bytes 280
  2.7 0.0 copy-done.7
  2.8 0.0 copy-done.8
  2.8 0.0 copy-start.4
  2.8 0.1 pad_maximum_fusion.prm_ref
  2.9 0.7 %copy-done.4 = bf16[256,64]{0,1:T(8,128)(2,1)S(1)} copy-done((bf16[256,64]{0,1:T(8,128)(2,1)S(1)}, bf16[256,64]{0,1:T(8,128)(2,1)}, u32[]{:S(2)}) %copy-start.4) | copy-done | bytes 32792
  3.6 0.0 copy-start.2
  3.6 0.0 copy-start.3
  3.6 0.1 copy.19.wp_ref
  3.7 0.6 %copy-done.2 = bf16[64,256]{1,0:T(8,128)(2,1)S(1)} copy-done((bf16[64,256]{1,0:T(8,128)(2,1)S(1)}, bf16[64,256]{1,0:T(8,128)(2,1)}, u32[]{:S(2)}) %copy-start.2) | copy-done | bytes 32792
  4.3 0.0 copy-done.3
  4.3 0.0 copy-start
  4.3 1.0 %copy-done = bf16[64,8,270]{2,1,0:T(8,128)(2,1)S(1)} copy-done((bf16[64,8,270]{2,1,0:T(8,128)(2,1)S(1)}, bf16[64,8,270]{2,1,0:T(8,128)(2,1)}, u32[]{:S(2)}) %copy-start) | copy-done | bytes 276504
  5.3 0.0 copy-start.1
  5.3 1.0 %copy-done.1 = bf16[64,8,270]{2,1,0:T(8,128)(2,1)S(1)} copy-done((bf16[64,8,270]{2,1,0:T(8,128)(2,1)S(1)}, bf16[64,8,270]{2,1,0:T(8,128)(2,1)}, u32[]{:S(2)}) %copy-start.1) | copy-done | bytes 276504
  6.3 46.0 %shard_map.169 = (bf16[64,8,270]{2,1,0:T(8,128)(2,1)S(1)}, f32[64,256]{1,0:T(8,128)S(1)}, f32[256,64]{1,0:T(8,128)S(1)}, f32[32,128]{1,0:T(8,128)S(1)}) custom-call(bf16[64,8,270]{2,1,0:T(8,128)(2,1)S(1)} %copy-done, bf16[64,8,270]{2,1,0:T(8,128)(2,1)S(1)} %copy-done.1, s32[8,270]{1,0:T(8,128)S(1)} %copy-done.3, f32[56,128]{1,0:T(8,128)S(1)} %pad_maximum_fusion.prm_ref, ...), custom_call_target="tpu_custom_call" | custom-call | tf_op jit(solution)/shard_map/pallas_call | solution.py:600
  52.3 0.6 %slice_bitcast_fusion = f32[256]{0:T(256)} fusion(f32[32,128]{1,0:T(8,128)S(1)} %get-tuple-element.14), kind=kLoop, calls=%fused_computation.3 | loop fusion | bytes 2048 | tf_op jit(solution)/shard_map/reshape | solution.py:668
  52.8 0.6 %slice_bitcast_fusion.1 = (f32[64]{0:T(128)}, f32[64]{0:T(128)}, f32[64]{0:T(128)}, f32[64]{0:T(128)}) fusion(f32[32,128]{1,0:T(8,128)S(1)} %get-tuple-element.14), kind=kLoop, calls=%fused_computation.4 | loop fusion | bytes 2048 | tf_op jit(solution)/shard_map/squeeze | solution.py:670
  53.4 0.1 slice.22
  53.5 0.6 %reshape.28 = f32[64,7,7]{0,2,1:T(8,128)} reshape(f32[64,49]{0,1:T(8,128)S(1)} %maximum_bitcast_fusion) | data formatting | bytes 25088 | tf_op jit(solution)/shard_map/reshape | solution.py:660
  54.1 0.7 %copy.20 = f32[256,64]{0,1:T(8,128)} copy(f32[256,64]{1,0:T(8,128)S(1)} %get-tuple-element.24) | data formatting | bytes 131072
  54.8 0.7 %copy.23 = bf16[64,8,270]{2,1,0:T(8,128)(2,1)} copy(bf16[64,8,270]{2,1,0:T(8,128)(2,1)S(1)} %get-tuple-element.39) | data formatting | bytes 552960
  55.6 0.6 %copy.24 = f32[64,256]{1,0:T(8,128)} copy(f32[64,256]{1,0:T(8,128)S(1)} %get-tuple-element.44) | data formatting | bytes 131072
  (4 shorter events, 0.0 us)
Async XLA Ops:
  0.6 0.7 %copy-start.5 = (f32[256]{0:T(256)S(1)}, f32[256]{0:T(256)}, u32[]{:S(2)}) copy-start(f32[256]{0:T(256)} %param.18) | copy-start | bytes 3076
  2.1 0.7 %copy-start.6 = (f32[64]{0:T(128)S(1)}, f32[64]{0:T(128)}, u32[]{:S(2)}) copy-start(f32[64]{0:T(128)} %param.14) | copy-start | bytes 772
  2.1 0.7 %copy-start.7 = (f32[64]{0:T(128)S(1)}, f32[64]{0:T(128)}, u32[]{:S(2)}) copy-start(f32[64]{0:T(128)} %param.15) | copy-start | bytes 772
  2.1 0.7 %copy-start.8 = (f32[64]{0:T(128)S(1)}, f32[64]{0:T(128)}, u32[]{:S(2)}) copy-start(f32[64]{0:T(128)} %param.16) | copy-start | bytes 772
  2.8 0.8 %copy-start.4 = (bf16[256,64]{0,1:T(8,128)(2,1)S(1)}, bf16[256,64]{0,1:T(8,128)(2,1)}, u32[]{:S(2)}) copy-start(bf16[256,64]{0,1:T(8,128)(2,1)} %param.19) | copy-start | bytes 98308
  3.6 0.8 %copy-start.2 = (bf16[64,256]{1,0:T(8,128)(2,1)S(1)}, bf16[64,256]{1,0:T(8,128)(2,1)}, u32[]{:S(2)}) copy-start(bf16[64,256]{1,0:T(8,128)(2,1)} %we_ref.1) | copy-start | bytes 98308
  3.6 0.8 %copy-start.3 = (s32[8,270]{1,0:T(8,128)S(1)}, s32[8,270]{1,0:T(8,128)}, u32[]{:S(2)}) copy-start(s32[8,270]{1,0:T(8,128)} %land_ref.1) | copy-start | bytes 25924
  4.3 1.0 %copy-start = (bf16[64,8,270]{2,1,0:T(8,128)(2,1)S(1)}, bf16[64,8,270]{2,1,0:T(8,128)(2,1)}, u32[]{:S(2)}) copy-start(bf16[64,8,270]{2,1,0:T(8,128)(2,1)} %state_hbm.1) | copy-start | bytes 829444
  5.3 1.0 %copy-start.1 = (bf16[64,8,270]{2,1,0:T(8,128)(2,1)S(1)}, bf16[64,8,270]{2,1,0:T(8,128)(2,1)}, u32[]{:S(2)}) copy-start(bf16[64,8,270]{2,1,0:T(8,128)(2,1)} %cot_hbm.1) | copy-start | bytes 829444

commit v3 on v2

--- a/solution.py
+++ b/solution.py
@@ -20,12 +20,12 @@
 EXT_COLS = 144
 STEP = 272
 N_GROUP = 16
-CHUNK = 18
 MESH = pl.DeviceIdType.MESH
 
 ln_eps = 1e-06
 root_half = 0.7071067811865476
 inv_root_tau = 0.3989422804014327
+half_log2e = -0.7213475204444817
 
 f32 = jnp.float32
 bf16 = jnp.bfloat16
@@ -49,17 +49,27 @@
 def kernel_body(
     state_hbm,
     cot_hbm,
-    land_ref,
-    prm_ref,
-    be_ref,
-    we_ref,
-    wp_ref,
+    land_hbm,
+    kern_hbm,
+    cb_hbm,
+    gain_hbm,
+    lb_hbm,
+    we_hbm,
+    be_hbm,
+    wp_hbm,
     grad_ref,
-    expand_ref,
-    project_ref,
+    big_ref,
     small_ref,
     state_in,
     cot_in,
+    land_ref,
+    kern_ref,
+    cb_ref,
+    gain_ref,
+    lb_ref,
+    we_ref,
+    be_ref,
+    wp_ref,
     planes,
     turned,
     s_ext,
@@ -78,14 +88,17 @@
     wbd,
     wpbd,
     mean_ref,
+    mean2_ref,
     eg_ref,
     pg_ref,
     acc_ref,
     tap_out,
-    pay,
-    part,
-    gather,
-    total_ref,
+    pay_b,
+    part_b,
+    gather_b,
+    pay_s,
+    part_s,
+    gather_s,
     row_send,
     row_recv,
     col_send,
@@ -95,12 +108,18 @@
     row_rsem,
     col_ssem,
     col_rsem,
-    s1,
-    r1,
-    s2,
-    r2,
-    s3,
-    r3,
+    sb1,
+    rb1,
+    sb2,
+    rb2,
+    sb3,
+    rb3,
+    ss1,
+    rs1,
+    ss2,
+    rs2,
+    ss3,
+    rs3,
 ):
     la = lax.axis_index("lat")
     lo = lax.axis_index("lon")
@@ -109,10 +128,25 @@
     has_north = la > 0
     has_south = la < N_GROUP - 1
 
-    state_copy = pltpu.make_async_copy(state_hbm, state_in, in_sem.at[0])
-    state_copy.start()
-    cot_copy = pltpu.make_async_copy(cot_hbm, cot_in, in_sem.at[1])
-    cot_copy.start()
+    inputs = [
+        pltpu.make_async_copy(src, dst, in_sem.at[i])
+        for i, (src, dst) in enumerate(
+            (
+                (state_hbm, state_in),
+                (cot_hbm, cot_in),
+                (land_hbm, land_ref),
+                (kern_hbm, kern_ref),
+                (cb_hbm, cb_ref),
+                (gain_hbm, gain_ref),
+                (lb_hbm, lb_ref),
+                (we_hbm, we_ref),
+                (be_hbm, be_ref),
+                (wp_hbm, wp_ref),
+            )
+        )
+    ]
+    for copy in inputs:
+        copy.start()
 
     def lat_peer(k):
         return {"lat": lax.rem(la + k, N_GROUP), "lon": lo}
@@ -140,23 +174,6 @@
 
     lane = lax.broadcasted_iota(jnp.int32, (ROWS, 8, 128), 2)
     sub = lax.broadcasted_iota(jnp.int32, (ROWS, 8, 128), 1)
-
-    for i in range(TAPS * TAPS):
-        taps_ref[i] = jnp.broadcast_to(prm_ref[i : i + 1, :], (8, 128))
-    wbd[...] = jnp.zeros((128, 512), bf16)
-    wbd[0:64, 0:256] = we_ref[...]
-    wbd[64:128, 256:512] = we_ref[...]
-    nothing = jnp.zeros((EXPAND, CHAN), bf16)
-    wpbd[0:256, :] = jnp.concatenate([wp_ref[...], nothing], axis=1)
-    wpbd[256:512, :] = jnp.concatenate([nothing, wp_ref[...]], axis=1)
-    at_row = lax.broadcasted_iota(jnp.int32, (256, 128), 0)
-    at_col = lax.broadcasted_iota(jnp.int32, (256, 128), 1)
-    same = lax.rem(at_row, 128) // 64 == at_col // 64
-    mean_ref[...] = jnp.where(same, 1.0 / CHAN, 0.0).astype(bf16)
-
-    conv_bias = prm_ref[49:50, :]
-    gain = prm_ref[50:51, :]
-    ln_bias = prm_ref[51:52, :]
 
     s_ext[:, 136:144, :] = jnp.zeros((EXT_ROWS, 8, 128), f32)
     d_ext[:, 136:144, :] = jnp.zeros((EXT_ROWS, 8, 128), f32)
@@ -329,7 +346,7 @@
 
         lax.fori_loop(0, TILES, step, 0)
 
-    state_copy.wait()
+    inputs[0].wait()
     to_planes(lambda at: state_in[at].astype(f32))
 
     def put_state(r, value):
@@ -345,7 +362,8 @@
     )
     start_copies(0)
 
-    cot_copy.wait()
+    inputs[1].wait()
+    inputs[2].wait()
     land = land_ref[...].astype(f32)
     to_planes(lambda at: cot_in[at].astype(f32) * land[None])
 
@@ -355,8 +373,6 @@
 
     turn_in(put_wet)
     acc_ref[...] = jnp.zeros((5, 8, 512), f32)
-    eg_ref[...] = jnp.zeros((128, 512), f32)
-    pg_ref[...] = jnp.zeros((128, 512), f32)
 
     def narrow(i, carry):
         at = pl.ds(pl.multiple_of(i * 16, 16), 16)
@@ -366,6 +382,34 @@
 
     acc_ref[0, :, 0:128] = lax.fori_loop(0, CELLS // 16, narrow, jnp.zeros((8, 128), f32))
 
+    for copy in inputs[3:]:
+        copy.wait()
+    for a in range(TAPS):
+        for b in range(TAPS):
+            one = kern_ref[a, b : b + 1, :]
+            taps_ref[a * TAPS + b] = jnp.broadcast_to(
+                jnp.concatenate([one, one], axis=1), (8, 128)
+            )
+    wbd[...] = jnp.zeros((128, 512), bf16)
+    wbd[0:64, 0:256] = we_ref[...]
+    wbd[64:128, 256:512] = we_ref[...]
+    wpbd[...] = jnp.zeros((128, 512), bf16)
+    wpbd[0:64, 0:256] = wp_ref[...]
+    wpbd[64:128, 256:512] = wp_ref[...]
+    at_row = lax.broadcasted_iota(jnp.int32, (256, 256), 0) // 64
+    at_col = lax.broadcasted_iota(jnp.int32, (256, 256), 1) // 64
+    mean2_ref[...] = jnp.where(at_row == at_col, 1.0 / CHAN, 0.0).astype(bf16)
+    mean_ref[0:128, :] = mean2_ref[0:128, 0:128]
+    mean_ref[128:256, :] = mean2_ref[0:128, 0:128]
+
+    def twice(ref):
+        return jnp.concatenate([ref[...], ref[...]], axis=1)
+
+    conv_bias = twice(cb_ref)
+    gain = twice(gain_ref)
+    ln_bias = twice(lb_ref)
+    be = twice(be_ref)
+
     finish_copies(s_ext, 0)
     convolve(s_ext, False, conv_bias)
 
@@ -376,22 +420,23 @@
         at = pl.ds(pl.multiple_of(q * STEP, STEP), STEP)
         x = x_ref[at, :]
         cen = x - dot(split(x), mean_ref[...], NN)
-        rstd = lax.rsqrt(dot(split(cen * cen), mean_ref[...], NN) + ln_eps)
+        var = dot((cen * cen).astype(bf16), mean_ref[0:128, :], NN)
+        rstd = lax.rsqrt(var + ln_eps)
         normed = cen * rstd
         zed = (normed * gain + ln_bias).astype(bf16)
         norm_ref[...] = normed
         rstd_ref[...] = rstd
-        zed_ref[...] = zed
+        zed_ref[at, :] = zed
         pre_ref[...] = dot(zed, wbd[...], NN)
-        wet = wet16[at, :]
-        dact_ref[...] = dot(wet, wpbd[...], NT)
+        dact_ref[...] = dot(wet16[at, :], wpbd[...], NN)
 
         def gelu(i, total):
             rows = pl.ds(pl.multiple_of(i * 16, 16), 16)
+            to = pl.ds(pl.multiple_of(q * STEP + i * 16, 16), 16)
             for k in range(4):
                 cols = slice(128 * k, 128 * k + 128)
-                pre = pre_ref[rows, cols] + be_ref[0:1, cols]
-                grow = jnp.exp(-0.5 * pre * pre)
+                pre = pre_ref[rows, cols] + be[:, cols]
+                grow = jnp.exp2(pre * pre * half_log2e)
                 t = 1.0 / (1.0 + (0.3275911 * root_half) * jnp.abs(pre))
                 poly = 0.5 * 1.061405429 * t - 0.5 * 1.453152027
                 poly = poly * t + 0.5 * 1.421413741
@@ -400,30 +445,91 @@
                 tail = poly * t * grow
                 phi = jnp.where(pre >= 0, 1.0 - tail, tail)
                 slope = phi + pre * grow * inv_root_tau
-                act_ref[rows, cols] = (pre * phi).astype(bf16)
+                act_ref[to, cols] = (pre * phi).astype(bf16)
                 dhid = (dact_ref[rows, cols] * slope).astype(bf16)
-                dhid_ref[rows, cols] = dhid
+                dhid_ref[to, cols] = dhid
                 wide = dhid.astype(f32)
                 acc_ref[1, :, cols] += wide[0:8] + wide[8:16]
             return total
 
         lax.fori_loop(0, STEP // 16, gelu, 0)
-        dhid = dhid_ref[...]
-        dzed = dot(dhid, wbd[...], NT)
+        dzed = dot(dhid_ref[at, :], wbd[...], NT)
         normed = norm_ref[...]
         acc_ref[2, :, 0:128] += fold(dzed * normed)
         acc_ref[3, :, 0:128] += fold(dzed)
         dnorm = dzed * gain
-        m1 = dot(split(dnorm), mean_ref[...], NN)
-        m2 = dot(split(dnorm * normed), mean_ref[...], NN)
-        dconv = rstd_ref[...] * (dnorm - m1 - normed * m2)
+        both = jnp.concatenate([dnorm.astype(bf16), (dnorm * normed).astype(bf16)], axis=1)
+        means = dot(both, mean2_ref[...], NN)
+        dconv = rstd_ref[...] * (dnorm - means[:, 0:128] - normed * means[:, 128:256])
         x_ref[at, :] = dconv
         acc_ref[4, :, 0:128] += fold(dconv)
-        eg_ref[...] += dot(zed_ref[...], dhid, TN)
-        pg_ref[...] += dot(wet16[at, :], act_ref[...], TN)
         return carry
 
     lax.fori_loop(0, CELLS // STEP, pointwise, 0)
+    eg_ref[...] = dot(zed_ref[...], dhid_ref[...], TN)
+    pg_ref[...] = dot(wet16[...], act_ref[...], TN)
+
+    def halves(x):
+        return x + pltpu.roll(x, 64, axis=1)
+
+    for i in range(N_GROUP):
+        c, e = 8 * (i // 2), 128 * (i % 2)
+        one, two = [
+            ref[c : c + 8, e : e + 128] + ref[64 + c : 72 + c, 256 + e : 384 + e]
+            for ref in (eg_ref, pg_ref)
+        ]
+        pay_b[i] = jnp.concatenate([one, two], axis=0).astype(bf16)
+
+    def scatter(pay, part, ssem, rsem):
+        copies = []
+        for k in range(1, N_GROUP):
+            copies.append(
+                pltpu.make_async_remote_copy(
+                    src_ref=pay.at[lax.rem(la + k, N_GROUP)],
+                    dst_ref=part.at[k],
+                    send_sem=ssem.at[k],
+                    recv_sem=rsem.at[k],
+                    device_id=lat_peer(k),
+                    device_id_type=MESH,
+                )
+            )
+            copies[-1].start()
+        return copies
+
+    def spread(ref, at, peer, ssem, rsem):
+        copies = []
+        for k in range(1, N_GROUP):
+            copies.append(
+                pltpu.make_async_remote_copy(
+                    src_ref=ref.at[at],
+                    dst_ref=ref.at[at],
+                    send_sem=ssem.at[k],
+                    recv_sem=rsem.at[k],
+                    device_id=peer(k),
+                    device_id_type=MESH,
+                )
+            )
+            copies[-1].start()
+        return copies
+
+    def scattered(pay, part, gather, copies):
+        total = pay[la].astype(f32)
+        for k in range(1, N_GROUP):
+            copies[k - 1].wait()
+            total = total + part[k].astype(f32)
+        gather[lo] = total.astype(gather.dtype)
+
+    scale = 1.0 / math.sqrt(ROWS * N_GROUP * COLS * N_GROUP)
+
+    def gathered(gather, out, copies):
+        for copy in copies:
+            copy.wait()
+        total = gather[0].astype(f32)
+        for k in range(1, N_GROUP):
+            total = total + gather[k].astype(f32)
+        out[la] = (total * scale).astype(out.dtype)
+
+    copies_b = scatter(pay_b, part_b, sb1, rb1)
 
     def place(r, carry):
         d_ext[r + 3, 3 : 3 + PITCH, :] = x_ref[pl.ds(pl.multiple_of(r * PITCH, 8), PITCH), :]
@@ -452,18 +558,7 @@
         for a in range(TAPS):
             tap_out[a * TAPS + b] = acc[a]
 
-    def halves(x):
-        return x + pltpu.roll(x, 64, axis=1)
-
     first_half = lax.broadcasted_iota(jnp.int32, (1, 128), 1) < 64
-    for i in range(N_GROUP):
-        c, e = 8 * (i // 2), 128 * (i % 2)
-        pay[i, 0:8, :] = (
-            eg_ref[c : c + 8, e : e + 128] + eg_ref[64 + c : 72 + c, 256 + e : 384 + e]
-        )
-        pay[i, 8:16, :] = (
-            pg_ref[c : c + 8, e : e + 128] + pg_ref[64 + c : 72 + c, 256 + e : 384 + e]
-        )
 
     def sums_of(x):
         return halves(jnp.sum(x, axis=0, keepdims=True))
@@ -486,42 +581,18 @@
     while len(rows) < 32:
         rows.append(jnp.zeros((1, 128), f32))
     for i in range(N_GROUP):
-        pay[i, 16:17, :] = rows[2 * i]
-        pay[i, 17:18, :] = rows[2 * i + 1]
-
-    copies1 = []
-    for k in range(1, N_GROUP):
-        copy = pltpu.make_async_remote_copy(
-            src_ref=pay.at[lax.rem(la + k, N_GROUP)],
-            dst_ref=part.at[k],
-            send_sem=s1.at[k],
-            recv_sem=r1.at[k],
-            device_id=lat_peer(k),
-            device_id_type=MESH,
-        )
-        copy.start()
-        copies1.append(copy)
+        pay_s[i, 0:1, :] = rows[2 * i]
+        pay_s[i, 1:2, :] = rows[2 * i + 1]
+
+    copies_s = scatter(pay_s, part_s, ss1, rs1)
+    scattered(pay_b, part_b, gather_b, copies_b)
+    copies_b = spread(gather_b, lo, lon_peer, sb2, rb2)
 
     finish_copies(d_ext, 1)
     convolve(d_ext, True, None)
 
-    total = pay[la]
-    for k in range(1, N_GROUP):
-        copies1[k - 1].wait()
-        total = total + part[k]
-    gather[lo] = total
-    copies2 = []
-    for k in range(1, N_GROUP):
-        copy = pltpu.make_async_remote_copy(
-            src_ref=gather.at[lo],
-            dst_ref=gather.at[lo],
-            send_sem=s2.at[k],
-            recv_sem=r2.at[k],
-            device_id=lon_peer(k),
-            device_id_type=MESH,
-        )
-        copy.start()
-        copies2.append(copy)
+    scattered(pay_s, part_s, gather_s, copies_s)
+    copies_s = spread(gather_s, lo, lon_peer, ss2, rs2)
 
     def turn_out(p, carry):
         r = p * 2
@@ -549,67 +620,87 @@
 
     lax.fori_loop(0, 8, write_out, 0)
 
-    for copy in copies2:
+    gathered(gather_b, big_ref, copies_b)
+    copies_b = spread(big_ref, la, lat_peer, sb3, rb3)
+    gathered(gather_s, small_ref, copies_s)
+    copies_s = spread(small_ref, la, lat_peer, ss3, rs3)
+    for copy in copies_b + copies_s:
         copy.wait()
-    total = gather[0]
-    for k in range(1, N_GROUP):
-        total = total + gather[k]
-    scale = 1.0 / math.sqrt(ROWS * N_GROUP * COLS * N_GROUP)
-    total_ref[la] = total * scale
-    copies3 = []
-    for k in range(1, N_GROUP):
-        copy = pltpu.make_async_remote_copy(
-            src_ref=total_ref.at[la],
-            dst_ref=total_ref.at[la],
-            send_sem=s3.at[k],
-            recv_sem=r3.at[k],
-            device_id=lat_peer(k),
-            device_id_type=MESH,
-        )
-        copy.start()
-        copies3.append(copy)
-    for copy in copies3:
-        copy.wait()
-
-    for e in range(2):
-        pieces = []
-        for c in range(8):
-            i = 2 * c + e
-            expand_ref[8 * c : 8 * c + 8, 128 * e : 128 * e + 128] = total_ref[i, 0:8, :]
-            pieces.append(total_ref[i, 8:16, :])
-        pieces.append(jnp.zeros((64, 128), f32))
-        project_ref[128 * e : 128 * e + 128, :] = jnp.concatenate(pieces, axis=0).T[:, 0:64]
+
+
+def finish(
+    grad_ref,
+    big_ref,
+    small_ref,
+    grad_hbm,
+    kern_out,
+    cb_out,
+    gain_out,
+    lb_out,
+    expand_out,
+    be_out,
+    project_out,
+    bp_out,
+    rows_ref,
+    sem,
+):
+    copy = pltpu.make_async_copy(grad_ref, grad_hbm, sem)
+    copy.start()
     for i in range(N_GROUP):
-        small_ref[2 * i : 2 * i + 2, :] = total_ref[i, 16:18, :]
+        c, e = 8 * (i // 2), 128 * (i % 2)
+        both = big_ref[i].astype(f32)
+        expand_out[c : c + 8, e : e + 128] = both[0:8]
+        project_out[c : c + 8, e : e + 128] = both[8:16]
+    for i in range(N_GROUP):
+        rows_ref[2 * i : 2 * i + 2, :] = small_ref[i]
+    be_out[:, 0:128] = rows_ref[25:26, :]
+    be_out[:, 128:256] = rows_ref[26:27, :]
+    cb_out[...] = rows_ref[27:28, 0:64]
+    gain_out[...] = pltpu.roll(rows_ref[27:28, :], 64, axis=1)[:, 0:64]
+    lb_out[...] = rows_ref[28:29, 0:64]
+    bp_out[...] = pltpu.roll(rows_ref[28:29, :], 64, axis=1)[:, 0:64]
+    rows = rows_ref[0:32, :]
+    turned = pltpu.roll(rows, 64, axis=1)
+    for i in range(TAPS * TAPS):
+        a, b = i // TAPS, i % TAPS
+        of, at = (rows, i) if i < 25 else (turned, i - 25)
+        kern_out[a, b : b + 1, :] = of[at : at + 1, 0:64]
+    copy.wait()
+
+
+def far(x):
+    return pltpu.with_memory_space_constraint(x, pltpu.HBM)
 
 
 def body(
     state, land_sea, cotangent, kernel, conv_bias, ln_gain, ln_bias, w_expand, b_expand, w_project
 ):
-    taps = kernel.reshape(CHAN, TAPS * TAPS).T
-    prm = jnp.concatenate(
-        [taps, conv_bias[None], ln_gain[None], ln_bias[None], jnp.zeros((4, CHAN), f32)], axis=0
-    )
-    prm = jnp.concatenate([prm, prm], axis=1)
-    be = jnp.concatenate([b_expand, b_expand])[None]
     vmem = pl.BlockSpec(memory_space=pltpu.VMEM)
-    anyw = pl.BlockSpec(memory_space=pl.ANY)
+    hbm = pl.BlockSpec(memory_space=pltpu.HBM)
     sds = jax.ShapeDtypeStruct
     sem = pltpu.SemaphoreType.DMA
-    piece = (N_GROUP, CHUNK, 128)
-    grad, expand, project, small = pl.pallas_call(
+    big = (N_GROUP, 16, 128)
+    small = (N_GROUP, 2, 128)
+    grad, big_sums, small_sums = pl.pallas_call(
         kernel_body,
         out_shape=(
             sds((CHAN, ROWS, COLS), bf16),
-            sds((CHAN, EXPAND), f32),
-            sds((EXPAND, CHAN), f32),
-            sds((32, 128), f32),
+            sds(big, bf16),
+            sds(small, f32),
         ),
-        in_specs=[anyw, anyw, vmem, vmem, vmem, vmem, vmem],
-        out_specs=(vmem, vmem, vmem, vmem),
+        in_specs=[hbm] * 10,
+        out_specs=(vmem, vmem, vmem),
         scratch_shapes=[
             pltpu.VMEM((CHAN, ROWS, COLS), bf16),
             pltpu.VMEM((CHAN, ROWS, COLS), bf16),
+            pltpu.VMEM((ROWS, COLS), jnp.int32),
+            pltpu.VMEM((TAPS, TAPS, CHAN), f32),
+            pltpu.VMEM((1, CHAN), f32),
+            pltpu.VMEM((1, CHAN), f32),
+            pltpu.VMEM((1, CHAN), f32),
+            pltpu.VMEM((CHAN, EXPAND), bf16),
+            pltpu.VMEM((1, EXPAND), f32),
+            pltpu.VMEM((CHAN, EXPAND), bf16),
             pltpu.VMEM((3, CHAN * ROWS, 128), f32),
             pltpu.VMEM((384, 128), f32),
             pltpu.VMEM((EXT_ROWS, EXT_COLS, 128), f32),
@@ -619,56 +710,84 @@
             pltpu.VMEM((CELLS, 128), f32),
             pltpu.VMEM((STEP, 128), f32),
             pltpu.VMEM((STEP, 128), f32),
-            pltpu.VMEM((STEP, 128), bf16),
+            pltpu.VMEM((CELLS, 128), bf16),
             pltpu.VMEM((STEP, 512), f32),
             pltpu.VMEM((STEP, 512), f32),
-            pltpu.VMEM((STEP, 512), bf16),
-            pltpu.VMEM((STEP, 512), bf16),
+            pltpu.VMEM((CELLS, 512), bf16),
+            pltpu.VMEM((CELLS, 512), bf16),
             pltpu.VMEM((TAPS * TAPS, 8, 128), f32),
             pltpu.VMEM((128, 512), bf16),
-            pltpu.VMEM((512, 128), bf16),
+            pltpu.VMEM((128, 512), bf16),
             pltpu.VMEM((256, 128), bf16),
+            pltpu.VMEM((256, 256), bf16),
             pltpu.VMEM((128, 512), f32),
             pltpu.VMEM((128, 512), f32),
             pltpu.VMEM((5, 8, 512), f32),
             pltpu.VMEM((TAPS * TAPS, 8, 128), f32),
-            pltpu.VMEM(piece, f32),
-            pltpu.VMEM(piece, f32),
-            pltpu.VMEM(piece, f32),
-            pltpu.VMEM(piece, f32),
+            pltpu.VMEM(big, bf16),
+            pltpu.VMEM(big, bf16),
+            pltpu.VMEM(big, bf16),
+            pltpu.VMEM(small, f32),
+            pltpu.VMEM(small, f32),
+            pltpu.VMEM(small, f32),
             pltpu.VMEM((2, 2, 3, EXT_COLS, 128), bf16),
             pltpu.VMEM((2, 2, 3, EXT_COLS, 128), bf16),
             pltpu.VMEM((2, 2, ROWS, 8, 128), f32),
             pltpu.VMEM((2, 2, EXT_ROWS, 8, 128), f32),
-            sem((2,)),
+            sem((10,)),
             sem((2, 2)),
             sem((2, 2)),
             sem((2, 2, 3)),
             sem((2, 2, 3)),
-            sem((N_GROUP,)),
-            sem((N_GROUP,)),
-            sem((N_GROUP,)),
-            sem((N_GROUP,)),
-            sem((N_GROUP,)),
-            sem((N_GROUP,)),
-        ],
+        ]
+        + [sem((N_GROUP,))] * 12,
         compiler_params=pltpu.CompilerParams(
             collective_id=0, has_side_effects=True, vmem_limit_bytes=48 * 2**20
         ),
-    )(state, cotangent, land_sea, prm, be, w_expand, w_project)
-    tap_rows = jnp.concatenate([small[0:25, 0:64], small[0:24, 64:128]], axis=0)
-    kernel_grad = tap_rows.T.reshape(CHAN, TAPS, TAPS)
-    return (
-        grad,
-        kernel_grad,
-        small[27, 0:64],
-        small[27, 64:128],
-        small[28, 0:64],
-        expand,
-        small[25:27].reshape(EXPAND),
-        project,
-        small[28, 64:128],
+    )(
+        *map(
+            far,
+            (
+                state,
+                cotangent,
+                land_sea,
+                kernel.transpose(1, 2, 0),
+                conv_bias[None],
+                ln_gain[None],
+                ln_bias[None],
+                w_expand,
+                b_expand[None],
+                w_project.T,
+            ),
+        )
     )
+    outs = pl.pallas_call(
+        finish,
+        out_shape=(
+            sds((CHAN, ROWS, COLS), bf16),
+            sds((TAPS, TAPS, CHAN), f32),
+            sds((1, CHAN), f32),
+            sds((1, CHAN), f32),
+            sds((1, CHAN), f32),
+            sds((CHAN, EXPAND), f32),
+            sds((1, EXPAND), f32),
+            sds((CHAN, EXPAND), f32),
+            sds((1, CHAN), f32),
+        ),
+        in_specs=[vmem] * 3,
+        out_specs=(hbm,) + (vmem,) * 8,
+        scratch_shapes=[
+            pltpu.VMEM((32, 128), f32),
+            sem(()),
+        ],
+        compiler_params=pltpu.CompilerParams(vmem_limit_bytes=8 * 2**20),
+    )(grad, big_sums, small_sums)
+    outs = list(outs)
+    outs[1] = outs[1].transpose(2, 0, 1)
+    outs[7] = outs[7].T
+    for i in (2, 3, 4, 6, 8):
+        outs[i] = outs[i].reshape(-1)
+    return tuple(outs)
 
 
 def solution(mesh):

time: 56.6 us -> 47 us (0.83)
  local copies, waits for them, and re-layouts: 9.47 us -> 0 us
    unnamed x22 -> x0, local copies, waits for them, and re-layouts: 6.85 us -> none
    reshape x3 -> x0, local copies, waits for them, and re-layouts: 1.93 us -> none  [the longest x1 0.75 us: body(): taps = kernel.reshape(CHAN, TAPS * TAPS).T]
    pallas_call x0 -> x1, Pallas kernels: none -> 1.44 us  [body(): pl.pallas_call(finish, out_shape=(sds((CHAN, ROWS, COLS), bf16), sds((TAP...]
    pallas_call x1, Pallas kernels: 46 us -> 44.8 us  [body(): pl.pallas_call(kernel_body, out_shape=(sds((CHAN, ROWS, COLS), bf16), sds...]
    squeeze x1 -> x0, local copies, waits for them, and re-layouts: 0.59 us -> none  [body(): small[28, 64:128]]
where the time goes in v3:
time: 47 us; the launch traced here: 46.9 us
  Pallas kernels  46.3 us (99%)
  between operations  0.65 us (1%)
    pallas_call x1, Pallas kernels, body(): pl.pallas_call(kernel_body, out_shape=(sds((CHAN, ROWS, COLS), bf16), sds...  44.8 us
    pallas_call x1, Pallas kernels, body(): pl.pallas_call(finish, out_shape=(sds((CHAN, ROWS, COLS), bf16), sds((TAP...  1.44 us

profile of v3, /device:TPU:1, one launch (start us, length us, event | category | flops | bytes accessed | tf_op | source)
XLA Modules:
  0.0 46.9 jit_solution(12508150926244687479)
XLA Ops:
  0.6 44.8 %shard_map.169 = (bf16[64,8,270]{2,1,0:T(8,128)(2,1)S(1)}, bf16[16,16,128]{2,1,0:T(8,128)(2,1)S(1)}, f32[16,2,128]{2,1,0:T(2,128)S(1)}) custom-call(bf16[64,8,270]{2,1,0:T(8,128)(2,1)} %state_hbm.1, bf16[64,8,270]{2,1,0:T(8,128)(2,1)} %cot_hbm.1, s32[8,270]{1,0:T(8,128)} %land_hbm.1, f32[7,7,64]{2,1,0:T(8,128)} %bitcast.14, f32[1,64]{1,0:T(1,128)} %bitcast.16, ...), custom_call_target="tpu_custom_call" | custom-call | tf_op jit(solution)/shard_map/pallas_call | solution.py:684
  45.5 1.4 %shard_map.170 = (bf16[64,8,270]{2,1,0:T(8,128)(2,1)}, f32[7,7,64]{2,1,0:T(8,128)}, f32[1,64]{1,0:T(1,128)}, f32[1,64]{1,0:T(1,128)}, f32[1,64]{1,0:T(1,128)}, /...) custom-call(bf16[64,8,270]{2,1,0:T(8,128)(2,1)S(1)} %get-tuple-element.21.grad_ref, ...), custom_call_target="tpu_custom_call" | custom-call | tf_op jit(solution)/shard_map/pallas_call | solution.py:764

commit v4 on v3

--- a/solution.py
+++ b/solution.py
@@ -19,6 +19,9 @@
 EXT_ROWS = 14
 EXT_COLS = 144
 STEP = 272
+PART = 544
+GROUP = 32
+BACK = 544
 N_GROUP = 16
 MESH = pl.DeviceIdType.MESH
 
@@ -103,6 +106,7 @@
     row_recv,
     col_send,
     col_recv,
+    hello_sem,
     in_sem,
     row_ssem,
     row_rsem,
@@ -155,7 +159,7 @@
         return {"lat": la, "lon": lax.rem(lo + k, N_GROUP)}
 
     barrier = pltpu.get_barrier_semaphore()
-    for k in range(1, N_GROUP):
+    for k in (1, N_GROUP - 1):
         pl.semaphore_signal(barrier, inc=1, device_id=lat_peer(k), device_id_type=MESH)
         pl.semaphore_signal(barrier, inc=1, device_id=lon_peer(k), device_id_type=MESH)
     for side in (east, west):
@@ -171,6 +175,19 @@
             pl.semaphore_signal(
                 barrier, inc=1, device_id={"lat": la + 1, "lon": side}, device_id_type=MESH
             )
+
+    def hello(n):
+        for k in (2**n, N_GROUP - 2**n):
+            pl.semaphore_signal(
+                hello_sem.at[0, n], inc=1, device_id=lat_peer(k), device_id_type=MESH
+            )
+            pl.semaphore_signal(
+                hello_sem.at[1, n], inc=1, device_id=lon_peer(k), device_id_type=MESH
+            )
+
+    def heard(n):
+        pl.semaphore_wait(hello_sem.at[0, n], 2)
+        pl.semaphore_wait(hello_sem.at[1, n], 2)
 
     lane = lax.broadcasted_iota(jnp.int32, (ROWS, 8, 128), 2)
     sub = lax.broadcasted_iota(jnp.int32, (ROWS, 8, 128), 1)
@@ -329,22 +346,33 @@
         def _():
             fill(11, 14)
 
-    def convolve(ext, flip, bias):
+    def convolve(ext, flip, bias, tiles, stride, part=0):
         def step(t, carry):
-            at = pl.multiple_of(t * 8, 8)
-            acc = jnp.zeros((ROWS, 8, 128), f32)
-            if bias is not None:
-                acc = acc + bias[None]
+            at = pl.multiple_of(t * (8 * stride) + 8 * (stride == 1), 8)
+            if part == 2:
+                acc = [x_ref[pl.ds(at + r * PITCH, 8), :] for r in range(ROWS)]
+            else:
+                first = jnp.zeros((8, 128), f32)
+                if bias is not None:
+                    first = first + bias
+                acc = [first] * ROWS
             for b in range(TAPS):
-                x = ext[:, pl.ds(at + b, 8), :]
+                rows = {
+                    i: ext[i, pl.ds(at + b, 8), :]
+                    for i in range(EXT_ROWS)
+                    if part == 0 or (part == 1) == (3 <= i < 11)
+                }
                 for a in range(TAPS):
                     i = a * TAPS + b
-                    acc = acc + taps_ref[48 - i if flip else i][None] * x[a : a + ROWS]
+                    tap = taps_ref[48 - i if flip else i]
+                    for r in range(ROWS):
+                        if r + a in rows:
+                            acc[r] = acc[r] + tap * rows[r + a]
             for r in range(ROWS):
                 x_ref[pl.ds(at + r * PITCH, 8), :] = acc[r]
             return carry
 
-        lax.fori_loop(0, TILES, step, 0)
+        lax.fori_loop(0, tiles, step, 0)
 
     inputs[0].wait()
     to_planes(lambda at: state_in[at].astype(f32))
@@ -356,11 +384,12 @@
     exchange(s_ext, 0)
     pl.semaphore_wait(
         barrier,
-        2 * (N_GROUP - 1)
+        4
         + 2 * has_north.astype(jnp.int32)
         + 2 * has_south.astype(jnp.int32),
     )
     start_copies(0)
+    hello(0)
 
     inputs[1].wait()
     inputs[2].wait()
@@ -410,62 +439,77 @@
     ln_bias = twice(lb_ref)
     be = twice(be_ref)
 
+    heard(0)
+    hello(1)
+
+    def back(q, carry):
+        at = pl.ds(pl.multiple_of(q * STEP, STEP), STEP)
+        dact_ref[at, :] = dot(wet16[at, :], wpbd[...], NN)
+        return carry
+
+    lax.fori_loop(0, CELLS // STEP, back, 0)
+    convolve(s_ext, False, conv_bias, TILES - 2, 1, 1)
+    heard(1)
+    hello(2)
     finish_copies(s_ext, 0)
-    convolve(s_ext, False, conv_bias)
+    convolve(s_ext, False, conv_bias, TILES - 2, 1, 2)
+    convolve(s_ext, False, conv_bias, 2, TILES - 1)
 
     def fold(x):
         return jnp.sum(x.reshape(-1, 8, x.shape[-1]), axis=0)
 
-    def pointwise(q, carry):
-        at = pl.ds(pl.multiple_of(q * STEP, STEP), STEP)
+    def forward(q, carry):
+        at = pl.ds(pl.multiple_of(q * PART, PART), PART)
         x = x_ref[at, :]
         cen = x - dot(split(x), mean_ref[...], NN)
         var = dot((cen * cen).astype(bf16), mean_ref[0:128, :], NN)
         rstd = lax.rsqrt(var + ln_eps)
         normed = cen * rstd
         zed = (normed * gain + ln_bias).astype(bf16)
-        norm_ref[...] = normed
-        rstd_ref[...] = rstd
+        norm_ref[at, :] = normed
+        rstd_ref[at, :] = rstd
         zed_ref[at, :] = zed
-        pre_ref[...] = dot(zed, wbd[...], NN)
-        dact_ref[...] = dot(wet16[at, :], wpbd[...], NN)
-
-        def gelu(i, total):
-            rows = pl.ds(pl.multiple_of(i * 16, 16), 16)
-            to = pl.ds(pl.multiple_of(q * STEP + i * 16, 16), 16)
-            for k in range(4):
-                cols = slice(128 * k, 128 * k + 128)
-                pre = pre_ref[rows, cols] + be[:, cols]
-                grow = jnp.exp2(pre * pre * half_log2e)
-                t = 1.0 / (1.0 + (0.3275911 * root_half) * jnp.abs(pre))
-                poly = 0.5 * 1.061405429 * t - 0.5 * 1.453152027
-                poly = poly * t + 0.5 * 1.421413741
-                poly = poly * t - 0.5 * 0.284496736
-                poly = poly * t + 0.5 * 0.254829592
-                tail = poly * t * grow
-                phi = jnp.where(pre >= 0, 1.0 - tail, tail)
-                slope = phi + pre * grow * inv_root_tau
-                act_ref[to, cols] = (pre * phi).astype(bf16)
-                dhid = (dact_ref[rows, cols] * slope).astype(bf16)
-                dhid_ref[to, cols] = dhid
-                wide = dhid.astype(f32)
-                acc_ref[1, :, cols] += wide[0:8] + wide[8:16]
-            return total
-
-        lax.fori_loop(0, STEP // 16, gelu, 0)
+        pre_ref[at, :] = dot(zed, wbd[...], NN)
+        return carry
+
+    lax.fori_loop(0, CELLS // PART, forward, 0)
+
+    def gelu(i, total):
+        rows = pl.ds(pl.multiple_of(i * GROUP, GROUP), GROUP)
+        for k in range(4):
+            cols = slice(128 * k, 128 * k + 128)
+            pre = pre_ref[rows, cols] + be[:, cols]
+            grow = jnp.exp2(pre * pre * half_log2e)
+            t = 1.0 / (1.0 + (0.3275911 * root_half) * jnp.abs(pre))
+            poly = 0.5 * 1.061405429 * t - 0.5 * 1.453152027
+            poly = poly * t + 0.5 * 1.421413741
+            poly = poly * t - 0.5 * 0.284496736
+            poly = poly * t + 0.5 * 0.254829592
+            tail = poly * t * grow
+            phi = jnp.where(pre >= 0, 1.0 - tail, tail)
+            slope = phi + pre * grow * inv_root_tau
+            act_ref[rows, cols] = (pre * phi).astype(bf16)
+            dhid = (dact_ref[rows, cols] * slope).astype(bf16)
+            dhid_ref[rows, cols] = dhid
+            acc_ref[1, :, cols] += fold(dhid.astype(f32))
+        return total
+
+    lax.fori_loop(0, CELLS // GROUP, gelu, 0)
+
+    def backward(q, carry):
+        at = pl.ds(pl.multiple_of(q * BACK, BACK), BACK)
         dzed = dot(dhid_ref[at, :], wbd[...], NT)
-        normed = norm_ref[...]
+        normed = norm_ref[at, :]
         acc_ref[2, :, 0:128] += fold(dzed * normed)
         acc_ref[3, :, 0:128] += fold(dzed)
         dnorm = dzed * gain
         both = jnp.concatenate([dnorm.astype(bf16), (dnorm * normed).astype(bf16)], axis=1)
         means = dot(both, mean2_ref[...], NN)
-        dconv = rstd_ref[...] * (dnorm - means[:, 0:128] - normed * means[:, 128:256])
+        dconv = rstd_ref[at, :] * (dnorm - means[:, 0:128] - normed * means[:, 128:256])
         x_ref[at, :] = dconv
         acc_ref[4, :, 0:128] += fold(dconv)
         return carry
 
-    lax.fori_loop(0, CELLS // STEP, pointwise, 0)
     eg_ref[...] = dot(zed_ref[...], dhid_ref[...], TN)
     pg_ref[...] = dot(wet16[...], act_ref[...], TN)
 
@@ -529,34 +573,29 @@
             total = total + gather[k].astype(f32)
         out[la] = (total * scale).astype(out.dtype)
 
+    heard(2)
     copies_b = scatter(pay_b, part_b, sb1, rb1)
-
-    def place(r, carry):
-        d_ext[r + 3, 3 : 3 + PITCH, :] = x_ref[pl.ds(pl.multiple_of(r * PITCH, 8), PITCH), :]
-        return carry
-
-    lax.fori_loop(0, ROWS, place, 0)
-    exchange(d_ext, 1)
-    start_copies(1)
-
-    for b in range(TAPS):
+    lax.fori_loop(0, CELLS // BACK, backward, 0)
+
+    for group in ((0, 1, 2), (3, 4), (5, 6)):
 
         def tap_step(t, acc):
             at = pl.multiple_of(t * 8, 8)
-            x = s_ext[:, pl.ds(at + b, 8), :]
             d = [x_ref[pl.ds(at + r * PITCH, 8), :] for r in range(ROWS)]
-            new = []
+            new = list(acc)
+            for n, b in enumerate(group):
+                for i in range(EXT_ROWS):
+                    x = s_ext[i, pl.ds(at + b, 8), :]
+                    for a in range(TAPS):
+                        if 0 <= i - a < ROWS:
+                            new[n * TAPS + a] = new[n * TAPS + a] + d[i - a] * x
+            return tuple(new)
+
+        zero = jnp.zeros((8, 128), f32)
+        acc = lax.fori_loop(0, TILES, tap_step, (zero,) * (TAPS * len(group)))
+        for n, b in enumerate(group):
             for a in range(TAPS):
-                s = acc[a]
-                for r in range(ROWS):
-                    s = s + d[r] * x[r + a]
-                new.append(s)
-            return tuple(new)
-
-        zero = jnp.zeros((8, 128), f32)
-        acc = lax.fori_loop(0, TILES, tap_step, (zero,) * TAPS)
-        for a in range(TAPS):
-            tap_out[a * TAPS + b] = acc[a]
+                tap_out[a * TAPS + b] = acc[n * TAPS + a]
 
     first_half = lax.broadcasted_iota(jnp.int32, (1, 128), 1) < 64
 
@@ -585,14 +624,24 @@
         pay_s[i, 1:2, :] = rows[2 * i + 1]
 
     copies_s = scatter(pay_s, part_s, ss1, rs1)
+    def place(r, carry):
+        d_ext[r + 3, 3 : 3 + PITCH, :] = x_ref[pl.ds(pl.multiple_of(r * PITCH, 8), PITCH), :]
+        return carry
+
+    lax.fori_loop(0, ROWS, place, 0)
+    exchange(d_ext, 1)
+    start_copies(1)
+
     scattered(pay_b, part_b, gather_b, copies_b)
     copies_b = spread(gather_b, lo, lon_peer, sb2, rb2)
-
-    finish_copies(d_ext, 1)
-    convolve(d_ext, True, None)
-
     scattered(pay_s, part_s, gather_s, copies_s)
     copies_s = spread(gather_s, lo, lon_peer, ss2, rs2)
+
+    finish_copies(d_ext, 1)
+    convolve(d_ext, True, None, 1, TILES)
+    convolve(d_ext, True, None, TILES - 1, 1)
+    gathered(gather_b, big_ref, copies_b)
+    copies_b = spread(big_ref, la, lat_peer, sb3, rb3)
 
     def turn_out(p, carry):
         r = p * 2
@@ -620,8 +669,6 @@
 
     lax.fori_loop(0, 8, write_out, 0)
 
-    gathered(gather_b, big_ref, copies_b)
-    copies_b = spread(big_ref, la, lat_peer, sb3, rb3)
     gathered(gather_s, small_ref, copies_s)
     copies_s = spread(small_ref, la, lat_peer, ss3, rs3)
     for copy in copies_b + copies_s:
@@ -708,11 +755,11 @@
             pltpu.VMEM((CELLS, 128), f32),
             pltpu.VMEM((CELLS, 128), bf16),
             pltpu.VMEM((CELLS, 128), f32),
-            pltpu.VMEM((STEP, 128), f32),
-            pltpu.VMEM((STEP, 128), f32),
+            pltpu.VMEM((CELLS, 128), f32),
+            pltpu.VMEM((CELLS, 128), f32),
             pltpu.VMEM((CELLS, 128), bf16),
-            pltpu.VMEM((STEP, 512), f32),
-            pltpu.VMEM((STEP, 512), f32),
+            pltpu.VMEM((CELLS, 512), f32),
+            pltpu.VMEM((CELLS, 512), f32),
             pltpu.VMEM((CELLS, 512), bf16),
             pltpu.VMEM((CELLS, 512), bf16),
             pltpu.VMEM((TAPS * TAPS, 8, 128), f32),
@@ -734,6 +781,7 @@
             pltpu.VMEM((2, 2, 3, EXT_COLS, 128), bf16),
             pltpu.VMEM((2, 2, ROWS, 8, 128), f32),
             pltpu.VMEM((2, 2, EXT_ROWS, 8, 128), f32),
+            pltpu.SemaphoreType.REGULAR((2, 3)),
             sem((10,)),
             sem((2, 2)),
             sem((2, 2)),

time: 47 us -> 43.3 us (0.921)
  Pallas kernels: 46.3 us -> 42.6 us
    pallas_call x1, Pallas kernels: 44.8 us -> 41.1 us  [body(): pl.pallas_call(kernel_body, out_shape=(sds((CHAN, ROWS, COLS), bf16), sds...]
where the time goes in v4:
time: 43.3 us; the launch traced here: 43.2 us
  Pallas kernels  42.6 us (98%)
  between operations  0.65 us (2%)
    pallas_call x1, Pallas kernels, body(): pl.pallas_call(kernel_body, out_shape=(sds((CHAN, ROWS, COLS), bf16), sds...  41.1 us
    pallas_call x1, Pallas kernels, body(): pl.pallas_call(finish, out_shape=(sds((CHAN, ROWS, COLS), bf16), sds((TAP...  1.44 us

profile of v4, /device:TPU:1, one launch (start us, length us, event | category | flops | bytes accessed | tf_op | source)
XLA Modules:
  0.0 43.2 jit_solution(15516505977900551147)
XLA Ops:
  0.6 41.1 %shard_map.169 = (bf16[64,8,270]{2,1,0:T(8,128)(2,1)S(1)}, bf16[16,16,128]{2,1,0:T(8,128)(2,1)S(1)}, f32[16,2,128]{2,1,0:T(2,128)S(1)}) custom-call(bf16[64,8,270]{2,1,0:T(8,128)(2,1)} %state_hbm.1, bf16[64,8,270]{2,1,0:T(8,128)(2,1)} %cot_hbm.1, s32[8,270]{1,0:T(8,128)} %land_hbm.1, f32[7,7,64]{2,1,0:T(8,128)} %bitcast.14, f32[1,64]{1,0:T(1,128)} %bitcast.16, ...), custom_call_target="tpu_custom_call" | custom-call | tf_op jit(solution)/shard_map/pallas_call | solution.py:731
  41.8 1.4 %shard_map.170 = (bf16[64,8,270]{2,1,0:T(8,128)(2,1)}, f32[7,7,64]{2,1,0:T(8,128)}, f32[1,64]{1,0:T(1,128)}, f32[1,64]{1,0:T(1,128)}, f32[1,64]{1,0:T(1,128)}, /...) custom-call(bf16[64,8,270]{2,1,0:T(8,128)(2,1)S(1)} %get-tuple-element.21.grad_ref, ...), custom_call_target="tpu_custom_call" | custom-call | tf_op jit(solution)/shard_map/pallas_call | solution.py:812
